TPU v7x, 32 devices: a whole 2x2x4 slice. The times are simulated.
32 devices in a mesh: atoms: 32 (over z, y, x, core).
Axes of the slice: x: 2, y: 2, z: 4, core: 2. Of those that a mesh axis runs over, the one named last changes fastest.
Arguments:
- features: bfloat16 [4096, 9, 128], P('atoms'), may hold values from -6 to 6
- cotangent: bfloat16 [4096, 9, 128], P('atoms'), may hold values from -6 to 6
- wigner: float32 [9, 9, 12288], P(None, None, 'atoms'), may hold values from -1 to 1, as said below
- pair_blocks: int32 [512, 2], P('atoms'), may hold values from 0 to 31, all different within a row; in each aligned block of 16 rows (0 to 15, 16 to 31, ...) at most 2 rows name the same one
- pair_rows: int32 [2, 6, 512], P(None, None, 'atoms'), may hold values from 0 to 127
- edge_ends: int32 [2, 12288], P(None, 'atoms'), may hold values from 0 to 5
- first_m0: bfloat16 [768, 512], replicated, may hold values from -0.21875 to 0.21875
- first_m1: bfloat16 [2, 512, 256], replicated, may hold values from -0.1875 to 0.1875
- first_m2: bfloat16 [2, 256, 128], replicated, may hold values from -0.25 to 0.25
- second_m0: bfloat16 [384, 384], replicated, may hold values from -0.3125 to 0.3125
- second_m1: bfloat16 [2, 256, 256], replicated, may hold values from -0.25 to 0.25
- second_m2: bfloat16 [2, 128, 128], replicated, may hold values from -0.375 to 0.375
Outputs:
- messages: bfloat16 [4096, 9, 128], P('atoms')
- grad_features: float32 [4096, 9, 128], P('atoms')
- grad_first_m0: float32 [768, 512], replicated
- grad_first_m1: float32 [2, 512, 256], replicated
- grad_first_m2: float32 [2, 256, 128], replicated
- grad_second_m0: float32 [384, 384], replicated
- grad_second_m1: float32 [2, 256, 256], replicated
- grad_second_m2: float32 [2, 128, 128], replicated
Inputs may be any that keep to these rules, and one draw needn't show every extreme that they name: `pair_blocks`: among the 16 pairs of one device no atom block is named more than 2 times; the two blocks of a pair differ. `wigner`: each edge's matrix is orthogonal and block diagonal over degrees 0, 1 and 2.
All inputs are finite; a program needn't handle non-finite values.
Results may differ from a plain program's by a relative error of at most 0.0045.
Values may be sent and summed in bfloat16 or wider, within the bound.
A program may use at most 128 MiB of HBM per device.

v0:
```python
import jax
import jax.numpy as jnp
from jax import lax
from jax.experimental import pallas as pl
from jax.experimental.pallas import tpu as pltpu
from jax.sharding import PartitionSpec as P

COEF_ORDER = (0, 2, 6, 3, 7, 1, 5, 8, 4)
DEGREES = ((0, 1), (1, 4), (4, 9))
CHUNK = 128
LANES = 128
VMEM_BYTES = 66_000_000


def degree_of(index):
    for low, high in DEGREES:
        if low <= index < high:
            return range(low, high)


def dot_nn(left, right):
    return jnp.dot(left, right, preferred_element_type=jnp.float32)


def dot_nt(left, right):
    return lax.dot_general(left, right, (((1,), (1,)), ((), ())), preferred_element_type=jnp.float32)


def dot_tn(left, right):
    return lax.dot_general(left, right, (((0,), (0,)), ((), ())), preferred_element_type=jnp.float32)


def pick_kernel(picked_ref, features_ref, cotangent_ref, out_ref):
    rows = out_ref.shape[0]
    coefs, atoms, channels = features_ref.shape
    chosen = picked_ref[...] == lax.broadcasted_iota(jnp.int32, (rows, atoms), 1)
    chosen = chosen.astype(jnp.float32).astype(jnp.bfloat16)
    for side, ref in enumerate((features_ref, cotangent_ref)):
        for j in range(coefs):
            at = (side * coefs + j) * channels
            out_ref[:, at : at + channels] = dot_nn(chosen, ref[j]).astype(jnp.bfloat16)


def owner_kernel(picked_ref, back_ref, messages_ref, grads_ref):
    rows = back_ref.shape[0]
    coefs, atoms, channels = grads_ref.shape
    chosen = picked_ref[...] == lax.broadcasted_iota(jnp.int32, (rows, atoms), 1)
    chosen = chosen.astype(jnp.float32).astype(jnp.bfloat16)
    for j in range(coefs):
        at = j * channels
        messages_ref[j] = dot_tn(chosen, back_ref[:, at : at + channels]).astype(jnp.bfloat16)
        at = (coefs + j) * channels
        grads_ref[j] = dot_tn(chosen, back_ref[:, at : at + channels])


def spread_kernel(packed_ref, *out_refs):
    at = 0
    for ref in out_refs:
        views = [ref] if len(ref.shape) == 2 else [ref.at[0], ref.at[1]]
        for view in views:
            height, width = view.shape
            for col in range(0, width, LANES):
                view[:, col : col + LANES] = packed_ref[at : at + height, :].astype(jnp.float32)
                at += height


def widen_into(ref, pair_ref):
    rows, cols = pair_ref.shape[1], pair_ref.shape[2]
    ref[:rows, :cols] = pair_ref[0]
    ref[:rows, cols:] = pair_ref[1]
    ref[rows:, :cols] = (-pair_ref[1].astype(jnp.float32)).astype(jnp.bfloat16)
    ref[rows:, cols:] = pair_ref[0]


def edge_kernel(
    flat_ref, wig_ref, pos_ref, fa0, fa1, fa2, sb0, sb1, sb2,
    slots_ref, packed_ref,
    acc, wa1, wa2, wb1, wb2, ga0, ga1, ga2, gb0, gb1, gb2,
    got, z, hid, gate_ref, act, mixed, dmix, dout, dz, contrib,
):
    C = LANES
    n_slots = flat_ref.shape[0]
    edges = wig_ref.shape[0]
    half = 9 * C
    widen_into(wa1, fa1)
    widen_into(wa2, fa2)
    widen_into(wb1, sb1)
    widen_into(wb2, sb2)
    for ref in (acc, ga0, ga1, ga2, gb0, gb1, gb2):
        ref[...] = jnp.zeros_like(ref)

    def step(index, carry):
        base = pl.multiple_of(index * CHUNK, CHUNK)
        span = pl.ds(base, CHUNK)
        slot_ids = lax.broadcasted_iota(jnp.int32, (CHUNK, n_slots), 1)

        def one_hot(which):
            hit = pos_ref[span, which : which + 1] == slot_ids
            return hit.astype(jnp.float32).astype(jnp.bfloat16)

        hot = jnp.concatenate([one_hot(0), one_hot(1)], axis=0)
        for c in range(0, 2 * half, 256):
            got[:, c : c + 256] = dot_nn(hot, flat_ref[:, c : c + 256])
        T, S = slice(0, CHUNK), slice(CHUNK, 2 * CHUNK)
        wig = wig_ref[span, :]

        def entry(row, col):
            k = row * 9 + col
            return jnp.broadcast_to(wig[:, k : k + 1], (CHUNK, C))

        for i, o in enumerate(COEF_ORDER):
            sums = [None] * 4
            for j in degree_of(o):
                w = entry(o, j)
                parts = (
                    got[T, j * C : (j + 1) * C],
                    got[S, j * C : (j + 1) * C],
                    got[T, half + j * C : half + (j + 1) * C],
                    got[S, half + j * C : half + (j + 1) * C],
                )
                sums = [w * p if s is None else s + w * p for s, p in zip(sums, parts)]
            rt, rs, ct, cs = (s.astype(jnp.bfloat16) for s in sums)
            left = slice(2 * i * C, (2 * i + 1) * C)
            right = slice((2 * i + 1) * C, (2 * i + 2) * C)
            z[T, left] = rs
            z[T, right] = rt
            z[S, left] = rt
            z[S, right] = rs
            dmix[T, i * C : (i + 1) * C] = ct
            dmix[S, i * C : (i + 1) * C] = cs

        first = dot_nn(z[:, : 6 * C], fa0[...])
        hid[:, : 3 * C] = first[:, : 3 * C]
        gate_ref[...] = jax.nn.sigmoid(first[:, 3 * C :])
        hid[:, 3 * C : 7 * C] = dot_nn(z[:, 6 * C : 14 * C], wa1[...])
        hid[:, 7 * C :] = dot_nn(z[:, 14 * C :], wa2[...])
        gate = gate_ref[...]
        h0 = hid[:, :C]
        act[:, :C] = (h0 * jax.nn.sigmoid(h0)).astype(jnp.bfloat16)
        for k in range(1, 9):
            act[:, k * C : (k + 1) * C] = (hid[:, k * C : (k + 1) * C] * gate).astype(jnp.bfloat16)
        mixed[:, : 3 * C] = dot_nn(act[:, : 3 * C], sb0[...])
        mixed[:, 3 * C : 7 * C] = dot_nn(act[:, 3 * C : 7 * C], wb1[...])
        mixed[:, 7 * C :] = dot_nn(act[:, 7 * C :], wb2[...])

        gb0[...] += dot_tn(act[:, : 3 * C], dmix[:, : 3 * C])
        gb1[...] += dot_tn(act[:, 3 * C : 7 * C], dmix[:, 3 * C : 7 * C])
        gb2[...] += dot_tn(act[:, 7 * C :], dmix[:, 7 * C :])
        dact = dz
        dact[:, : 3 * C] = dot_nt(dmix[:, : 3 * C], sb0[...])
        dact[:, 3 * C : 7 * C] = dot_nt(dmix[:, 3 * C : 7 * C], wb1[...])
        dact[:, 7 * C : 9 * C] = dot_nt(dmix[:, 7 * C :], wb2[...])
        head = jax.nn.sigmoid(h0)
        dout[:, :C] = (dact[:, :C] * head * (1.0 + h0 * (1.0 - head))).astype(jnp.bfloat16)
        grad_gate = None
        for k in range(1, 9):
            d = dact[:, k * C : (k + 1) * C]
            term = d * hid[:, k * C : (k + 1) * C]
            grad_gate = term if grad_gate is None else grad_gate + term
            at = k * C if k < 3 else (k + 1) * C
            dout[:, at : at + C] = (d * gate).astype(jnp.bfloat16)
        dout[:, 3 * C : 4 * C] = (grad_gate * gate * (1.0 - gate)).astype(jnp.bfloat16)

        ga0[...] += dot_tn(z[:, : 6 * C], dout[:, : 4 * C])
        ga1[...] += dot_tn(z[:, 6 * C : 14 * C], dout[:, 4 * C : 8 * C])
        ga2[...] += dot_tn(z[:, 14 * C :], dout[:, 8 * C :])
        dz[:, : 6 * C] = dot_nt(dout[:, : 4 * C], fa0[...])
        dz[:, 6 * C : 14 * C] = dot_nt(dout[:, 4 * C : 8 * C], wa1[...])
        dz[:, 14 * C :] = dot_nt(dout[:, 8 * C :], wa2[...])

        for j in range(9):
            sums = [None] * 4
            for i, o in enumerate(COEF_ORDER):
                if o not in degree_of(j):
                    continue
                w = entry(o, j)
                left = slice(2 * i * C, (2 * i + 1) * C)
                right = slice((2 * i + 1) * C, (2 * i + 2) * C)
                parts = (
                    mixed[T, i * C : (i + 1) * C],
                    mixed[S, i * C : (i + 1) * C],
                    dz[T, right] + dz[S, left],
                    dz[T, left] + dz[S, right],
                )
                sums = [w * p if s is None else s + w * p for s, p in zip(sums, parts)]
            for row, col, value in (
                (0, j * C, sums[0]),
                (CHUNK, j * C, sums[1]),
                (0, half + j * C, sums[2]),
                (CHUNK, half + j * C, sums[3]),
            ):
                upper = value.astype(jnp.bfloat16)
                contrib[row : row + CHUNK, col : col + C] = upper
                contrib[2 * CHUNK + row : 3 * CHUNK + row, col : col + C] = (
                    value - upper.astype(jnp.float32)
                ).astype(jnp.bfloat16)
        hot_twice = jnp.concatenate([hot, hot], axis=0)
        for c in range(0, 2 * half, 256):
            acc[:, c : c + 256] += dot_tn(hot_twice, contrib[:, c : c + 256])
        return carry

    lax.fori_loop(0, edges // CHUNK, step, 0)
    slots_ref[...] = acc[...].astype(jnp.bfloat16)

    at = 0

    def put(value):
        nonlocal at
        height = value.shape[0]
        for col in range(0, value.shape[1], C):
            packed_ref[at : at + height, :] = value[:, col : col + C].astype(jnp.bfloat16)
            at += height

    def put_pair(ref):
        rows, cols = ref.shape[0] // 2, ref.shape[1] // 2
        put(ref[:rows, :cols] + ref[rows:, cols:])
        put(ref[:rows, cols:] - ref[rows:, :cols])

    put(ga0[...])
    put_pair(ga1)
    put_pair(ga2)
    put(gb0[...])
    put_pair(gb1)
    put_pair(gb2)
    rest = packed_ref.shape[0] - at
    if rest:
        packed_ref[at:, :] = jnp.zeros((rest, C), jnp.bfloat16)


def call(kernel, out_shape, scratch=(), flops=1_000_000):
    many = isinstance(out_shape, (tuple, list))
    whole = pl.BlockSpec(memory_space=pltpu.VMEM)

    def run(*operands):
        return pl.pallas_call(
            kernel,
            out_shape=out_shape,
            in_specs=[whole] * len(operands),
            out_specs=[whole] * len(out_shape) if many else whole,
            scratch_shapes=list(scratch),
            compiler_params=pltpu.CompilerParams(vmem_limit_bytes=VMEM_BYTES),
            cost_estimate=pl.CostEstimate(flops=flops, bytes_accessed=4_000_000, transcendentals=0),
        )(*operands)

    return run


def exchange(value):
    return lax.all_to_all(value, "atoms", split_axis=0, concat_axis=0, tiled=True)


def grouped(value, groups):
    return lax.all_to_all(
        value, "atoms", split_axis=0, concat_axis=0, tiled=True, axis_index_groups=groups
    )


def local(features, cotangent, wigner, pair_blocks, pair_rows, edge_ends, *weights):
    peers = lax.axis_size("atoms")
    atoms, coefs, channels = features.shape
    pair_count = pair_blocks.shape[0]
    row_width = pair_rows.shape[1]
    edges = edge_ends.shape[1]
    per_pair = edges // pair_count
    slot_count = max(2, 4 * pair_count // peers)
    width = slot_count * row_width
    padded = -(-width // 16) * 16
    both = 2 * coefs * channels
    f32, bf16 = jnp.float32, jnp.bfloat16

    owners = pair_blocks.reshape(2 * pair_count)
    spots = jnp.arange(2 * pair_count, dtype=jnp.int32)
    rank = jnp.sum(
        (owners[:, None] == owners[None, :]) & (spots[:, None] > spots[None, :]), axis=1
    ).astype(jnp.int32)
    end_rows = jnp.transpose(pair_rows, (2, 0, 1)).reshape(2 * pair_count, row_width)
    place = owners * slot_count + rank
    names = jnp.arange(peers * slot_count, dtype=jnp.int32)
    request = jnp.sum(
        jnp.where((place[None, :] == names[:, None])[:, :, None], end_rows[None], 0), axis=1
    ).astype(jnp.int32)
    requested = exchange(request.reshape(peers, width))
    picked = jnp.pad(requested, ((0, 0), (0, padded - width)), constant_values=-1)
    picked = picked.reshape(peers * padded, 1)

    n_slots = peers * padded
    chosen = call(pick_kernel, jax.ShapeDtypeStruct((n_slots, both), bf16))(
        picked, jnp.transpose(features, (1, 0, 2)), jnp.transpose(cotangent, (1, 0, 2))
    )
    flat = exchange(chosen.reshape(peers, padded, both)).reshape(n_slots, both)

    end_slot = (owners * padded + rank * row_width).reshape(pair_count, 1, 2)
    ends = jnp.broadcast_to(end_slot, (pair_count, per_pair, 2)).reshape(edges, 2)
    positions = ends + jnp.transpose(edge_ends)
    wig = jnp.transpose(wigner.reshape(coefs * coefs, edges))

    total_rows = sum(w.size for w in weights) // LANES
    share = -(-total_rows // (16 * peers)) * 16
    rows = 2 * CHUNK
    V = pltpu.VMEM
    first_m0, first_m1, first_m2, second_m0, second_m1, second_m2 = weights
    wide = [(2 * w.shape[1], 2 * w.shape[2]) for w in (first_m1, first_m2, second_m1, second_m2)]
    scratch = [
        V((n_slots, both), f32),
        *[V(shape, bf16) for shape in wide],
        V(first_m0.shape, f32), V(wide[0], f32), V(wide[1], f32),
        V(second_m0.shape, f32), V(wide[2], f32), V(wide[3], f32),
        V((rows, both), f32),
        V((rows, both), bf16),
        V((rows, coefs * channels), f32),
        V((rows, channels), f32),
        V((rows, coefs * channels), bf16),
        V((rows, coefs * channels), f32),
        V((rows, coefs * channels), bf16),
        V((rows, (coefs + 1) * channels), bf16),
        V((rows, both), f32),
        V((2 * rows, both), bf16),
    ]
    slots, packed = call(
        edge_kernel,
        [
            jax.ShapeDtypeStruct((n_slots, both), bf16),
            jax.ShapeDtypeStruct((peers * share, LANES), bf16),
        ],
        scratch,
        flops=10_000_000_000,
    )(flat, wig, positions, *weights)

    grad_scale = (2.0 * edges * peers) ** (-0.5)
    back = exchange(slots.reshape(peers, padded, both)).reshape(n_slots, both)
    near_count = 8 if peers % 8 == 0 else 1
    far_count = peers // near_count
    near = [[h * near_count + n for n in range(near_count)] for h in range(far_count)]
    far = [[h * near_count + n for h in range(far_count)] for n in range(near_count)]
    parts = grouped(packed.reshape(near_count, far_count * share, LANES), near)
    block = jnp.sum(parts.astype(f32), axis=0).astype(bf16)
    parts = grouped(block.reshape(far_count, share, LANES), far)
    mine = (jnp.sum(parts.astype(f32), axis=0) * grad_scale).astype(bf16)
    block = grouped(jnp.broadcast_to(mine[None], (far_count, share, LANES)), far)
    block = block.reshape(1, far_count * share, LANES)
    everyone = grouped(jnp.broadcast_to(block, (near_count, far_count * share, LANES)), near)
    messages, grads = call(
        owner_kernel,
        [
            jax.ShapeDtypeStruct((coefs, atoms, channels), bf16),
            jax.ShapeDtypeStruct((coefs, atoms, channels), f32),
        ],
    )(picked, back)
    outs = call(spread_kernel, [jax.ShapeDtypeStruct(w.shape, f32) for w in weights])(
        everyone.reshape(peers * share, LANES)
    )
    return (jnp.transpose(messages, (1, 0, 2)), jnp.transpose(grads, (1, 0, 2)), *outs)


def solution(mesh):
    in_specs = (
        P("atoms", None, None),
        P("atoms", None, None),
        P(None, None, "atoms"),
        P("atoms", None),
        P(None, None, "atoms"),
        P(None, "atoms"),
        P(),
        P(),
        P(),
        P(),
        P(),
        P(),
    )
    out_specs = (P("atoms", None, None), P("atoms", None, None), P(), P(), P(), P(), P(), P())
    return jax.shard_map(local, mesh=mesh, in_specs=in_specs, out_specs=out_specs, check_vma=False)
```

profile of v0, /device:TPU:0, one launch (start us, length us, event | category | flops | bytes accessed | tf_op | source)
XLA Modules:
  0.0 246.4 jit_solution(825537115694171493)
XLA Ops:
  0.6 0.8 copy.53
  1.5 0.2 convert_reduce_fusion.1
  1.7 0.8 copy.54
  2.6 0.1 select_reduce_fusion
  2.7 0.1 copy.56
  2.9 14.3 %all_to_all.42 = s32[32,1,12]{2,1,0:T(1,128)S(1)} all-to-all(s32[32,1,12]{2,1,0:T(1,128)S(1)} %bitcast.29), channel_id=1, replica_groups=mesh['atoms'=32] {'atoms'}, dimensions={0} | all-to-all | bytes 3072 | tf_op jit(solution)/shard_map/all_to_all | solution.py:249
  17.2 0.9 reshape.110.picked_ref
  18.1 3.4 %shard_map.179 = bf16[512,2304]{1,0:T(8,128)(2,1)} custom-call(s32[512,1]{1,0:T(8,128)} %reshape.110.picked_ref, bf16[9,128,128]{2,1,0:T(8,128)(2,1)} %bitcast.26, bf16[9,128,128]{2,1,0:T(8,128)(2,1)} %bitcast.27), custom_call_target="tpu_custom_call" | custom-call | flops 1000000 | bytes 4000000 | tf_op jit(solution)/shard_map/pallas_call | solution.py:235
  21.5 3.6 %all-to-all-start.1 = ((bf16[32,16,2304]{2,1,0:T(8,128)(2,1)}), bf16[32,16,2304]{2,1,0:T(8,128)(2,1)}, u32[]{:S(2)}, u32[]{:S(2)}) async-start(bf16[32,16,2304]{2,1,0:T(8,128)(2,1)} %bitcast.21), calls=%async_computation.1 | async-start | bytes 4718592 | tf_op jit(solution)/shard_map/all_to_all | solution.py:249
  25.4 0.8 copy.59
  26.2 0.1 copy.62
  26.4 0.7 bitcast_add_fusion.pos_ref
  27.1 52.5 %all-to-all-done.1 = bf16[32,16,2304]{2,1,0:T(8,128)(2,1)} async-done(((bf16[32,16,2304]{2,1,0:T(8,128)(2,1)}), bf16[32,16,2304]{2,1,0:T(8,128)(2,1)}, u32[]{:S(2)}, u32[]{:S(2)}) %all-to-all-start.1) | async-done | bytes 2359328 | tf_op jit(solution)/shard_map/all_to_all | solution.py:249
  79.6 22.5 %shard_map.180 = (bf16[512,2304]{1,0:T(8,128)(2,1)}, bf16[8192,128]{1,0:T(8,128)(2,1)}) custom-call(bf16[512,2304]{1,0:T(8,128)(2,1)} %bitcast.7.flat_ref, f32[384,81]{1,0:T(8,128)} %bitcast.28, s32[384,2]{1,0:T(8,128)} %bitcast_add_fusion.pos_ref, bf16[768,512]{1,0:T(8,128)(2,1)} %fa0.1, bf16[2,512,256]{2,1,0:T(8,128)(2,1)} %fa1.1, ...), custom_call_target="tpu_custom_call" | custom-call | flops 10000000000 | bytes 4000000 | tf_op jit(solution)/shard_map/pallas_call | solution.py:235
  102.1 30.1 %all_to_all.43 = bf16[8,1024,128]{2,1,0:T(8,128)(2,1)S(1)} all-to-all(bf16[8,1024,128]{2,1,0:T(8,128)(2,1)} %bitcast.23), channel_id=1, replica_groups={{0,1,2,3,4,5,6,7},{8,9,10,11,12,13,14,15},{16,17,18,19,20,21,22,23},{24..., dimensions={0} | all-to-all | bytes 4194304 | tf_op jit(solution)/shard_map/all_to_all | solution.py:253
  132.2 0.4 reduce_sum.41
  132.6 11.2 %all_to_all.44 = bf16[4,256,128]{2,1,0:T(8,128)(2,1)S(1)} all-to-all(bf16[4,256,128]{2,1,0:T(8,128)(2,1)S(1)} %bitcast.24), channel_id=1, replica_groups={{0,8,16,24},{1,9,17,25},{2,10,18,26},{3,11,19,27},{4,12,20,28},{5,13,21..., dimensions={0} | all-to-all | bytes 524288 | tf_op jit(solution)/shard_map/all_to_all | solution.py:253
  143.9 11.0 %all_to_all.45 = bf16[4,256,128]{2,1,0:T(8,128)(2,1)S(1)} all-to-all(bf16[4,256,128]{2,1,0:T(8,128)(2,1)S(1)} %broadcast_in_dim.50), channel_id=1, replica_groups={{0,8,16,24},{1,9,17,25},{2,10,18,26},{3,11,19,27},{4,12,20,28},{5,13,21..., dimensions={0} | all-to-all | bytes 524288 | tf_op jit(solution)/shard_map/all_to_all | solution.py:253
  154.8 0.3 broadcast_in_dim.52
  155.1 29.7 %all_to_all.46 = bf16[8,1024,128]{2,1,0:T(8,128)(2,1)} all-to-all(bf16[8,1024,128]{2,1,0:T(8,128)(2,1)S(1)} %broadcast_in_dim.52), channel_id=1, replica_groups={{0,1,2,3,4,5,6,7},{8,9,10,11,12,13,14,15},{16,17,18,19,20,21,22,23},{24..., dimensions={0} | all-to-all | bytes 4194304 | tf_op jit(solution)/shard_map/all_to_all | solution.py:253
  184.8 3.5 %all-to-all-start.2 = ((bf16[32,16,2304]{2,1,0:T(8,128)(2,1)}), bf16[32,16,2304]{2,1,0:T(8,128)(2,1)}, u32[]{:S(2)}, u32[]{:S(2)}) async-start(bf16[32,16,2304]{2,1,0:T(8,128)(2,1)} %bitcast.11), calls=%async_computation.2 | async-start | bytes 4718592 | tf_op jit(solution)/shard_map/all_to_all | solution.py:249
  188.4 3.6 %shard_map.182 = (f32[768,512]{1,0:T(8,128)}, f32[2,512,256]{2,1,0:T(8,128)}, f32[2,256,128]{2,1,0:T(8,128)}, f32[384,384]{1,0:T(8,128)}, f32[2,256,256]{2,1,0:T(8,128)}, /*index=5*/f32[2,128,128]{2,1,0:T(8,128)}) custom-call(bf16[8192,128]{1,0:T(8,128)(2,1)} %bitcast.22), custom_call_target="tpu_custom_call" | custom-call | flops 1000000 | bytes 4000000 | tf_op jit(solution)/shard_map/pallas_call | solution.py:235
  192.0 50.9 %all-to-all-done.2 = bf16[32,16,2304]{2,1,0:T(8,128)(2,1)} async-done(((bf16[32,16,2304]{2,1,0:T(8,128)(2,1)}), bf16[32,16,2304]{2,1,0:T(8,128)(2,1)}, u32[]{:S(2)}, u32[]{:S(2)}) %all-to-all-start.2) | async-done | bytes 2359328 | tf_op jit(solution)/shard_map/all_to_all | solution.py:249
  242.9 3.6 %shard_map.181 = (bf16[9,128,128]{2,1,0:T(8,128)(2,1)}, f32[9,128,128]{2,1,0:T(8,128)}) custom-call(s32[512,1]{1,0:T(8,128)} %reshape.110.picked_ref, bf16[512,2304]{1,0:T(8,128)(2,1)} %bitcast.12.back_ref), custom_call_target="tpu_custom_call" | custom-call | flops 1000000 | bytes 4000000 | tf_op jit(solution)/shard_map/pallas_call | solution.py:235
  (20 shorter events, 0.7 us)
Async XLA Ops:
  21.5 3.8 %copy-start.1 = (s32[16,2]{0,1:T(2,128)S(1)}, s32[16,2]{0,1:T(2,128)}, u32[]{:S(2)}) copy-start(s32[16,2]{0,1:T(2,128)} %param.15) | copy-start | bytes 388
  21.5 3.9 %copy-start = (f32[9,9,384]{2,1,0:T(8,128)S(1)}, f32[9,9,384]{2,1,0:T(8,128)}, u32[]{:S(2)}) copy-start(f32[9,9,384]{2,1,0:T(8,128)} %param.14) | copy-start | bytes 373252
  21.5 4.8 %copy-start.2 = (s32[2,384]{1,0:T(2,128)S(1)}, s32[2,384]{1,0:T(2,128)}, u32[]{:S(2)}) copy-start(s32[2,384]{1,0:T(2,128)} %param.17) | copy-start | bytes 9220
  21.5 58.1 %all-to-all-start.1 = ((bf16[32,16,2304]{2,1,0:T(8,128)(2,1)}), bf16[32,16,2304]{2,1,0:T(8,128)(2,1)}, u32[]{:S(2)}, u32[]{:S(2)}) async-start(bf16[32,16,2304]{2,1,0:T(8,128)(2,1)} %bitcast.21), calls=%async_computation.1 | async-start | bytes 4718592 | tf_op jit(solution)/shard_map/all_to_all | solution.py:249
  184.8 58.0 %all-to-all-start.2 = ((bf16[32,16,2304]{2,1,0:T(8,128)(2,1)}), bf16[32,16,2304]{2,1,0:T(8,128)(2,1)}, u32[]{:S(2)}, u32[]{:S(2)}) async-start(bf16[32,16,2304]{2,1,0:T(8,128)(2,1)} %bitcast.11), calls=%async_computation.2 | async-start | bytes 4718592 | tf_op jit(solution)/shard_map/all_to_all | solution.py:249
where the time goes:
time: 247 us; the launch traced here: 246 us
  waiting for transfers between devices  103 us (42%)
  blocking collectives  96.3 us (39%)
  Pallas kernels  33.1 us (13%)
  starting transfers between devices  7.14 us (3%)
  local copies, waits for them, and re-layouts  4.32 us (2%)
    all_to_all x2, waiting for transfers between devices, exchange(): lax.all_to_all(value, 'atoms', split_axis=0, concat_axis=0, tiled=True)  103 us
    all_to_all x4, blocking collectives, grouped(): lax.all_to_all(value, 'atoms', split_axis=0, concat_axis=0, tiled=True, a...  82 us
    pallas_call x4, Pallas kernels, run(): pl.pallas_call(kernel, out_shape=out_shape, in_specs=[whole] * len(operan...  33.1 us
    all_to_all x1, blocking collectives, exchange(): lax.all_to_all(value, 'atoms', split_axis=0, concat_axis=0, tiled=True)  14.3 us
    all_to_all x2, starting transfers between devices, exchange(): lax.all_to_all(value, 'atoms', split_axis=0, concat_axis=0, tiled=True)  7.14 us
  transfers between devices with their start and end apart: 2, of which 2 were waited for; matrix products, arithmetic and copies ran while one was open for 1% of the time, Pallas kernels for 1%

commit v1 on v0

v1 whole, which is shorter than its diff:
```python
import jax
import jax.numpy as jnp
from jax import lax
from jax.experimental import pallas as pl
from jax.experimental.pallas import tpu as pltpu
from jax.sharding import PartitionSpec as P

COEF_ORDER = (0, 2, 6, 3, 7, 1, 5, 8, 4)
DEGREES = ((0, 1), (1, 4), (4, 9))
LANES = 128
TILE = 16
STREAMS = 4
AT_ONCE = 31
VMEM_BYTES = 66_000_000
MESH = pl.DeviceIdType.MESH
F32, BF16 = jnp.float32, jnp.bfloat16


def degree_of(index):
    for low, high in DEGREES:
        if low <= index < high:
            return range(low, high)


def dot_nn(left, right):
    return jnp.dot(left, right, preferred_element_type=F32)


def dot_nt(left, right):
    return lax.dot_general(left, right, (((1,), (1,)), ((), ())), preferred_element_type=F32)


def dot_tn(left, right):
    return lax.dot_general(left, right, (((0,), (0,)), ((), ())), preferred_element_type=F32)


def as_hot(hit):
    return hit.astype(F32).astype(BF16)


def tile_parts(coefs, width):
    tiles = -(-coefs * width // TILE)
    parts = []
    for t in range(tiles):
        first = TILE * t // width
        last = min((TILE * t + TILE - 1) // width, coefs - 1)
        assert last - first <= 1
        parts.append((first, last, TILE * t % width))
    return parts


def own_offsets(coefs, width):
    return [width * j % TILE for j in range(coefs)]


def unique(values):
    return sorted(set(values))


def widen_into(ref, pair_ref):
    rows, cols = pair_ref.shape[1], pair_ref.shape[2]
    ref[:rows, :cols] = pair_ref[0]
    ref[:rows, cols:] = pair_ref[1]
    ref[rows:, :cols] = (-pair_ref[1].astype(F32)).astype(BF16)
    ref[rows:, cols:] = pair_ref[0]


def spread_kernel(packed_ref, *out_refs):
    at = 0
    for ref in out_refs:
        views = [ref] if len(ref.shape) == 2 else [ref.at[0], ref.at[1]]
        for view in views:
            height, width = view.shape
            for col in range(0, width, LANES):
                view[:, col : col + LANES] = packed_ref[at : at + height, :].astype(F32)
                at += height


def main_kernel(width, pair_chunk, per_pair, grad_scale, peers, *refs):
    (
        req_ref, feat_ref, cot_ref, wig_ref, pos_ref, own_ref, fa0, fa1, fa2, sb0, sb1, sb2,
        msg_ref, grad_ref, fin,
        wa1, wa2, wb1, wb2,
        asked, hots, mine, send_f, send_c, recv_f, recv_c, back_m, back_g,
        pf, pc, am, ag,
        z, hid, gate_ref, act, dmix, dout, work, contrib,
        acc, snd, rcv,
        req_s, req_r, f_s, f_r, c_s, c_r, m_s, m_r, g_s, g_r, w_s, w_r,
    ) = refs
    shared = send_c is None
    send_c = send_f if shared else send_c
    C = LANES
    coefs, atoms, _ = feat_ref.shape
    half = coefs * C
    edges = wig_ref.shape[0]
    pair_rows = pf.shape[0]
    parts = tile_parts(coefs, width)
    starts = unique(p[2] for p in parts)
    offsets = own_offsets(coefs, width)
    kinds = unique(offsets)
    slots = peers * TILE
    me = lax.axis_index("atoms")

    barrier = pltpu.get_barrier_semaphore()

    def greet(k, carry):
        pl.semaphore_signal(barrier, inc=1, device_id=(lax.rem(me + k, peers),), device_id_type=MESH)
        return carry

    lax.fori_loop(1, peers, greet, 0)
    pl.semaphore_wait(barrier, peers - 1)

    def copies(source, target, send_sem, recv_sem):
        def at(k):
            to = lax.rem(me + k, peers)
            return pltpu.make_async_remote_copy(
                src_ref=source.at[to],
                dst_ref=target.at[me],
                send_sem=send_sem.at[k],
                recv_sem=recv_sem.at[k],
                device_id=(to,),
                device_id_type=MESH,
            )

        def start(first=1, last=peers):
            def go(k, carry):
                at(k).start()
                return carry

            lax.fori_loop(first, last, go, 0)

        def wait():
            def go(k, carry):
                at(k).wait()
                return carry

            lax.fori_loop(1, peers, go, 0)

        return start, wait

    start_req, wait_req = copies(req_ref, asked, req_s, req_r)
    start_req()
    asked[me] = req_ref[me]
    widen_into(wa1, fa1)
    widen_into(wa2, fa2)
    widen_into(wb1, sb1)
    widen_into(wb2, sb2)
    base = 0
    for m, off in enumerate(kinds):
        span = slots * (1 + (off + width - 1) // TILE)
        ids = lax.broadcasted_iota(jnp.int32, (pair_rows, span), 1)
        mine[:, base : base + span] = as_hot(own_ref[:, m : m + 1] == ids)
        base += span
    wait_req()

    rows_of = lax.broadcasted_iota(jnp.int32, (slots, peers), 0) // TILE
    chooser = as_hot(rows_of == lax.broadcasted_iota(jnp.int32, (slots, peers), 1))
    wanted = dot_nn(chooser, asked[...].reshape(peers, C).astype(BF16))
    lane = lax.broadcasted_iota(jnp.int32, (slots, C), 1)
    inner = lax.broadcasted_iota(jnp.int32, (slots, C), 0) % TILE
    atom_ids = lax.broadcasted_iota(jnp.int32, (slots, 2 * atoms), 1).astype(F32)
    for s in range(len(starts)):
        column = jnp.sum(jnp.where(lane == inner + s * TILE, wanted, 0.0), axis=1, keepdims=True)
        hots[s] = as_hot(column == atom_ids)

    def pick(block_ref, out_ref):
        for t, (first, last, start) in enumerate(parts):
            hot = hots.at[starts.index(start)]
            depth = (last - first + 1) * atoms
            table = block_ref[first : last + 1].reshape(depth, C)
            rows = dot_nn(hot[:, :depth], table).astype(BF16)
            out_ref[:, TILE * t : TILE * (t + 1), :] = rows.reshape(peers, TILE, C)

    start_f, wait_f = copies(send_f, recv_f, f_s, f_r)
    start_c, wait_c = copies(send_c, recv_c, c_s, c_r)
    pick(feat_ref, send_f)
    start_f()
    recv_f[me] = send_f[me]
    if shared:
        wait_f()
    pick(cot_ref, send_c)
    start_c()
    recv_c[me] = send_c[me]

    def own_hot(j):
        m = kinds.index(offsets[j])
        base = sum(slots * (1 + (off + width - 1) // TILE) for off in kinds[:m])
        tiles = 1 + (offsets[j] + width - 1) // TILE
        return base, tiles, width * j // TILE

    def gather(recv, out):
        for j in range(coefs):
            base, tiles, first = own_hot(j)
            total = None
            for h in range(tiles):
                hot = mine[:, base + h * slots : base + (h + 1) * slots]
                t = first + h
                rows = recv[:, TILE * t : TILE * (t + 1), :].reshape(slots, C)
                term = dot_nn(hot, rows)
                total = term if total is None else total + term
            out[:, j * C : (j + 1) * C] = total.astype(BF16)

    def scatter(sums, out):
        for t in range(len(parts)):
            total = None
            for j in range(parts[t][0], parts[t][1] + 1):
                base, tiles, first = own_hot(j)
                h = t - first
                assert 0 <= h < tiles
                hot = mine[:, base + h * slots : base + (h + 1) * slots]
                term = dot_tn(hot, sums[:, j * C : (j + 1) * C])
                total = term if total is None else total + term
            out[:, TILE * t : TILE * (t + 1), :] = total.astype(BF16).reshape(peers, TILE, C)

    chunk = pair_chunk * per_pair
    locals_ = pair_chunk * 2 * (pair_rows // (2 * (edges // per_pair)))
    T, S = slice(0, chunk), slice(chunk, 2 * chunk)

    def hot_of(index):
        span = pl.ds(pl.multiple_of(index * chunk, chunk), chunk)
        ids = lax.broadcasted_iota(jnp.int32, (chunk, locals_), 1)
        return jnp.concatenate(
            [as_hot(pos_ref[span, side : side + 1] == ids) for side in (0, 1)], axis=0
        )

    def table_of(ref, index):
        return ref.at[pl.ds(pl.multiple_of(index * locals_, locals_), locals_)]

    def entries(index):
        wig = wig_ref[pl.ds(pl.multiple_of(index * chunk, chunk), chunk), :]

        def entry(row, col):
            k = row * coefs + col
            return jnp.broadcast_to(wig[:, k : k + 1], (chunk, C))

        return entry

    def rotate(index, hot, table, put):
        rows = table_of(table, index)
        for c in range(0, half, 384):
            work[:, c : c + 384] = dot_nn(hot, rows[:, c : c + 384])
        entry = entries(index)
        for i, o in enumerate(COEF_ORDER):
            at_target = at_source = None
            for j in degree_of(o):
                w = entry(o, j)
                left = w * work[T, j * C : (j + 1) * C]
                right = w * work[S, j * C : (j + 1) * C]
                at_target = left if at_target is None else at_target + left
                at_source = right if at_source is None else at_source + right
            put(i, at_target.astype(BF16), at_source.astype(BF16))

    def unrotate(index, hot, take, out):
        entry = entries(index)
        for j in range(coefs):
            at_target = at_source = None
            for i, o in enumerate(COEF_ORDER):
                if o not in degree_of(j):
                    continue
                w = entry(o, j)
                left, right = take(i)
                left, right = w * left, w * right
                at_target = left if at_target is None else at_target + left
                at_source = right if at_source is None else at_source + right
            for row, value in ((0, at_target), (chunk, at_source)):
                contrib[row : row + chunk, j * C : (j + 1) * C] = value.astype(BF16)
        rows = table_of(out, index)
        for c in range(0, half, 384):
            rows[:, c : c + 384] = dot_tn(hot, contrib[:, c : c + 384]).astype(BF16)

    def all_rows(index):
        return pl.ds(pl.multiple_of(index * 2 * chunk, 2 * chunk), 2 * chunk)

    def forward(index, carry):
        hot = hot_of(index)
        zc, hc, gc, ac = (r.at[all_rows(index)] for r in (z, hid, gate_ref, act))

        def put(i, rt, rs):
            left = slice(2 * i * C, (2 * i + 1) * C)
            right = slice((2 * i + 1) * C, (2 * i + 2) * C)
            zc[T, left] = rs
            zc[T, right] = rt
            zc[S, left] = rt
            zc[S, right] = rs

        rotate(index, hot, pf, put)
        first = dot_nn(zc[:, : 6 * C], fa0[...])
        hc[:, : 3 * C] = first[:, : 3 * C]
        gc[...] = jax.nn.sigmoid(first[:, 3 * C :])
        hc[:, 3 * C : 7 * C] = dot_nn(zc[:, 6 * C : 14 * C], wa1[...])
        hc[:, 7 * C :] = dot_nn(zc[:, 14 * C :], wa2[...])
        gate = gc[...]
        h0 = hc[:, :C]
        ac[:, :C] = (h0 * jax.nn.sigmoid(h0)).astype(BF16)
        for k in range(1, 9):
            ac[:, k * C : (k + 1) * C] = (hc[:, k * C : (k + 1) * C] * gate).astype(BF16)
        work[:, : 3 * C] = dot_nn(ac[:, : 3 * C], sb0[...])
        work[:, 3 * C : 7 * C] = dot_nn(ac[:, 3 * C : 7 * C], wb1[...])
        work[:, 7 * C : 9 * C] = dot_nn(ac[:, 7 * C :], wb2[...])

        def take(i):
            col = slice(i * C, (i + 1) * C)
            return work[T, col], work[S, col]

        unrotate(index, hot, take, am)
        return carry

    def backward(index, carry):
        hot = hot_of(index)
        hc, gc, dc, oc = (r.at[all_rows(index)] for r in (hid, gate_ref, dmix, dout))

        def put(i, ct, cs):
            dc[T, i * C : (i + 1) * C] = ct
            dc[S, i * C : (i + 1) * C] = cs

        rotate(index, hot, pc, put)
        dact = work
        dact[:, : 3 * C] = dot_nt(dc[:, : 3 * C], sb0[...])
        dact[:, 3 * C : 7 * C] = dot_nt(dc[:, 3 * C : 7 * C], wb1[...])
        dact[:, 7 * C : 9 * C] = dot_nt(dc[:, 7 * C :], wb2[...])
        gate = gc[...]
        h0 = hc[:, :C]
        head = jax.nn.sigmoid(h0)
        oc[:, :C] = (dact[:, :C] * head * (1.0 + h0 * (1.0 - head))).astype(BF16)
        grad_gate = None
        for k in range(1, 9):
            d = dact[:, k * C : (k + 1) * C]
            term = d * hc[:, k * C : (k + 1) * C]
            grad_gate = term if grad_gate is None else grad_gate + term
            at = k * C if k < 3 else (k + 1) * C
            oc[:, at : at + C] = (d * gate).astype(BF16)
        oc[:, 3 * C : 4 * C] = (grad_gate * gate * (1.0 - gate)).astype(BF16)
        return carry

    def inputs_grad(index, carry):
        hot = hot_of(index)
        oc = dout.at[all_rows(index)]
        work[:, : 6 * C] = dot_nt(oc[:, : 4 * C], fa0[...])
        work[:, 6 * C : 14 * C] = dot_nt(oc[:, 4 * C : 8 * C], wa1[...])
        work[:, 14 * C :] = dot_nt(oc[:, 8 * C :], wa2[...])

        def take(i):
            left = slice(2 * i * C, (2 * i + 1) * C)
            right = slice((2 * i + 1) * C, (2 * i + 2) * C)
            return work[T, right] + work[S, left], work[T, left] + work[S, right]

        unrotate(index, hot, take, ag)
        return carry

    chunks = edges // chunk
    if not shared:
        wait_f()
    gather(recv_f, pf)
    lax.fori_loop(0, chunks, forward, 0)
    ret_m, ret_g = recv_f, recv_c
    start_m, wait_m = copies(ret_m, back_m, m_s, m_r)
    start_g, wait_g = copies(ret_g, back_g, g_s, g_r)
    scatter(am, ret_m)
    start_m()
    back_m[me] = ret_m[me]

    wait_c()
    gather(recv_c, pc)
    lax.fori_loop(0, chunks, backward, 0)

    at = 0

    def put(value):
        nonlocal at
        height = value.shape[0]
        for col in range(0, value.shape[1], C):
            acc[at // TILE : (at + height) // TILE] = value[:, col : col + C].reshape(height // TILE, TILE, C)
            at += height

    def weight_pair(left, right):
        rows, cols = left.shape[1] // 2, right.shape[1] // 2
        upper = dot_tn(left[:, :rows], right)
        lower = dot_tn(left[:, rows:], right)
        put(upper[:, :cols] + lower[:, cols:])
        put(upper[:, cols:] - lower[:, :cols])

    put(dot_tn(z[:, : 6 * C], dout[:, : 4 * C]))
    weight_pair(z[:, 6 * C : 14 * C], dout[:, 4 * C : 8 * C])
    weight_pair(z[:, 14 * C :], dout[:, 8 * C :])
    put(dot_tn(act[:, : 3 * C], dmix[:, : 3 * C]))
    weight_pair(act[:, 3 * C : 7 * C], dmix[:, 3 * C : 7 * C])
    weight_pair(act[:, 7 * C :], dmix[:, 7 * C :])
    blocks = acc.shape[0]
    if at < blocks * TILE:
        acc[at // TILE :] = jnp.zeros((blocks - at // TILE, TILE, C), F32)

    bits = peers.bit_length() - 1
    stream = blocks // STREAMS
    core = lax.rem(me, 2)
    strides = [2**b for b in range(bits)]
    if bits >= 3:
        strides[1] = 2 + 2 * core
        strides[2] = 4 - 2 * core
    low = [q * stream for q in range(STREAMS)]

    def w_copy(source, target, q, stage, stride):
        bit = lax.rem(me // stride, 2)
        return pltpu.make_async_remote_copy(
            src_ref=source,
            dst_ref=target,
            send_sem=w_s.at[stage * STREAMS + q],
            recv_sem=w_r.at[stage * STREAMS + q],
            device_id=(me + stride * (1 - 2 * bit),),
            device_id_type=MESH,
        )

    def halve_start(q, stage):
        size = stream >> (stage + 1)
        bit = lax.rem(me // strides[stage], 2)
        sent = low[q] + (1 - bit) * size
        low[q] = low[q] + bit * size
        snd[pl.ds(sent, size)] = acc[pl.ds(sent, size)].astype(BF16)
        landing = q * stream + stream - 2 * size
        copy = w_copy(snd.at[pl.ds(sent, size)], rcv.at[pl.ds(landing, size)], q, stage, strides[stage])
        copy.start()
        return copy, size, landing

    def halve_end(q, stage, state):
        copy, size, landing = state
        copy.wait()
        kept = pl.ds(low[q], size)
        total = acc[kept] + rcv[landing : landing + size].astype(F32)
        if stage == bits - 1:
            fin[kept] = (total * grad_scale).astype(BF16)
        else:
            acc[kept] = total

    def double_start(q, stage):
        size = stream >> (stage + 1)
        here = fin.at[pl.ds(low[q], size)]
        copy = w_copy(here, here, q, bits + stage, strides[stage])
        copy.start()
        return copy, size

    def double_end(q, stage, state):
        copy, size = state
        copy.wait()
        bit = lax.rem(me // strides[stage], 2)
        low[q] = low[q] - bit * size

    states = [halve_start(q, 0) for q in range(STREAMS)]

    def half_step(stage):
        for q in range(STREAMS):
            halve_end(q, stage, states[q])
            if stage + 1 < bits:
                states[q] = halve_start(q, stage + 1)
            else:
                states[q] = double_start(q, stage)
            send_some()

    def whole_step(stage):
        for q in range(STREAMS):
            double_end(q, stage, states[q])
            if stage:
                states[q] = double_start(q, stage - 1)
            send_some()

    sent = [0]

    def send_some():
        if sent[0]:
            last = min(peers, sent[0] + AT_ONCE * (peers - 1) // 31)
            start_g(sent[0], last)
            sent[0] = last

    for index in range(chunks):
        inputs_grad(index, 0)
        if index < bits - 1:
            half_step(index)
    scatter(ag, ret_g)
    back_g[me] = ret_g[me]
    sent[0] = 1
    send_some()
    for stage in range(min(chunks, bits - 1), bits):
        half_step(stage)

    def collect(back, out, dtype):
        for j in range(coefs):
            total = None
            for t, (first, last, start) in enumerate(parts):
                if not first <= j <= last:
                    continue
                hot = hots.at[starts.index(start)][:, (j - first) * atoms : (j - first + 1) * atoms]
                rows = back[:, TILE * t : TILE * (t + 1), :].reshape(slots, C)
                term = dot_tn(hot, rows)
                total = term if total is None else total + term
            out[j] = total.astype(dtype)

    stages = list(reversed(range(bits)))
    whole_step(stages[0])
    while sent[0] < peers:
        send_some()
    wait_m()
    collect(back_m, msg_ref, BF16)
    for stage in stages[1:]:
        whole_step(stage)
    wait_g()
    collect(back_g, grad_ref, F32)


def local(features, cotangent, wigner, pair_blocks, pair_rows, edge_ends, *weights):
    peers = lax.axis_size("atoms")
    atoms, coefs, channels = features.shape
    pair_count = pair_blocks.shape[0]
    row_width = pair_rows.shape[1]
    edges = edge_ends.shape[1]
    per_pair = edges // pair_count
    slot_count = max(2, 4 * pair_count // peers)
    width = slot_count * row_width
    half = coefs * channels
    bits = peers.bit_length() - 1

    owners = pair_blocks.reshape(2 * pair_count)
    spots = jnp.arange(2 * pair_count, dtype=jnp.int32)
    rank = jnp.sum(
        (owners[:, None] == owners[None, :]) & (spots[:, None] > spots[None, :]), axis=1
    ).astype(jnp.int32)
    end_rows = jnp.transpose(pair_rows, (2, 0, 1)).reshape(2 * pair_count, row_width)
    place = owners * slot_count + rank
    names = jnp.arange(peers * slot_count, dtype=jnp.int32)
    request = jnp.sum(
        jnp.where((place[None, :] == names[:, None])[:, :, None], end_rows[None], 0), axis=1
    ).astype(F32)
    request = request.reshape(peers, width)

    parts = tile_parts(coefs, width)
    starts = unique(p[2] for p in parts)
    pieces = []
    for start in starts:
        pieces.append(request[:, start:][:, :TILE])
        left = TILE - (width - start)
        if left > 0:
            pieces.append(request[:, :left] + float(atoms))
    asked = jnp.concatenate(pieces, axis=1)
    asked = jnp.pad(asked, ((0, 0), (0, LANES - asked.shape[1]))).reshape(peers, 1, LANES)

    kinds = unique(own_offsets(coefs, width))
    row_in_slot = rank[:, None] * row_width + jnp.arange(row_width, dtype=jnp.int32)[None, :]
    owned = []
    for off in kinds:
        at = row_in_slot + off
        owned.append((at // TILE) * (peers * TILE) + owners[:, None] * TILE + at % TILE)
    own = jnp.stack(owned, axis=-1).reshape(2 * pair_count * row_width, len(kinds))

    crowded = peers > 64
    pair_chunk = pair_count // (4 if crowded else 2)
    in_chunk = jnp.arange(edges, dtype=jnp.int32) // per_pair % pair_chunk * (2 * row_width)
    positions = jnp.transpose(edge_ends) + in_chunk[:, None]
    positions = positions + jnp.array([[0, row_width]], dtype=jnp.int32)
    wig = jnp.transpose(wigner.reshape(coefs * coefs, edges))

    total_rows = sum(w.size for w in weights) // LANES
    unit = TILE * peers * STREAMS
    packed_rows = -(-total_rows // unit) * unit
    rows = 2 * edges
    chunk_rows = 2 * pair_chunk * per_pair
    V, DMA = pltpu.VMEM, pltpu.SemaphoreType.DMA
    first_m0, first_m1, first_m2, second_m0, second_m1, second_m2 = weights
    wide = [(2 * w.shape[1], 2 * w.shape[2]) for w in (first_m1, first_m2, second_m1, second_m2)]
    slots = peers * TILE
    mine_width = sum(slots * (1 + (off + width - 1) // TILE) for off in kinds)
    block = (peers, TILE * len(parts), channels)
    end_count = 2 * pair_count * row_width
    packed_blocks = (packed_rows // TILE, TILE, LANES)
    scratch = [
        *[V(shape, BF16) for shape in wide],
        V((peers, 1, LANES), F32),
        V((len(starts), slots, 2 * atoms), BF16),
        V((end_count, mine_width), BF16),
        *[V(block, BF16) for _ in range(5 if crowded else 6)],
        *[V((end_count, half), BF16) for _ in range(4)],
        V((rows, 2 * half), BF16),
        V((rows, half), F32),
        V((rows, channels), F32),
        V((rows, half), BF16),
        V((rows, half), BF16),
        V((rows, half + channels), BF16),
        V((chunk_rows, 2 * half), F32),
        V((chunk_rows, half), BF16),
        V(packed_blocks, F32),
        V(packed_blocks, BF16),
        V(packed_blocks, BF16),
        *[DMA((peers,)) for _ in range(10)],
        DMA((2 * bits * STREAMS,)),
        DMA((2 * bits * STREAMS,)),
    ]
    whole = pl.BlockSpec(memory_space=pltpu.VMEM)
    first_block = 15 + 4 + 3
    grad_scale = (2.0 * edges * peers) ** (-0.5)

    def body(*refs):
        refs = list(refs)
        if crowded:
            refs.insert(first_block + 1, None)
        main_kernel(width, pair_chunk, per_pair, grad_scale, peers, *refs)

    operands = (
        asked, jnp.transpose(features, (1, 0, 2)), jnp.transpose(cotangent, (1, 0, 2)),
        wig, positions, own, *weights,
    )
    messages, grads, packed = pl.pallas_call(
        body,
        out_shape=[
            jax.ShapeDtypeStruct((coefs, atoms, channels), BF16),
            jax.ShapeDtypeStruct((coefs, atoms, channels), F32),
            jax.ShapeDtypeStruct(packed_blocks, BF16),
        ],
        in_specs=[whole] * len(operands),
        out_specs=[whole] * 3,
        scratch_shapes=scratch,
        compiler_params=pltpu.CompilerParams(
            collective_id=0, has_side_effects=True, vmem_limit_bytes=VMEM_BYTES
        ),
        name="edges",
    )(*operands)
    outs = pl.pallas_call(
        spread_kernel,
        out_shape=[jax.ShapeDtypeStruct(w.shape, F32) for w in weights],
        in_specs=[whole],
        out_specs=[whole] * len(weights),
        compiler_params=pltpu.CompilerParams(vmem_limit_bytes=VMEM_BYTES),
        name="spread",
    )(packed.reshape(packed_rows, LANES))
    return (jnp.transpose(messages, (1, 0, 2)), jnp.transpose(grads, (1, 0, 2)), *outs)


def solution(mesh):
    in_specs = (
        P("atoms", None, None),
        P("atoms", None, None),
        P(None, None, "atoms"),
        P("atoms", None),
        P(None, None, "atoms"),
        P(None, "atoms"),
        P(),
        P(),
        P(),
        P(),
        P(),
        P(),
    )
    out_specs = (P("atoms", None, None), P("atoms", None, None), P(), P(), P(), P(), P(), P())
    return jax.shard_map(local, mesh=mesh, in_specs=in_specs, out_specs=out_specs, check_vma=False)
```

time: 247 us -> 150 us (0.61)
  Pallas kernels: 33.1 us -> 140 us
  waiting for transfers between devices: 103 us -> 0 us
  blocking collectives: 96.3 us -> 0 us
  starting transfers between devices: 7.14 us -> 0 us
  local copies, waits for them, and re-layouts: 4.32 us -> 7.95 us
    pallas_call x4 -> x2, Pallas kernels: 33.1 us -> 140 us  [the longest x1 136 us: local(): pl.pallas_call(body, out_shape=[jax.ShapeDtypeStruct((coefs, atoms, chann...]
    all_to_all x2 -> x0, waiting for transfers between devices: 103 us -> none  [exchange(): lax.all_to_all(value, 'atoms', split_axis=0, concat_axis=0, tiled=True)]
    all_to_all x5 -> x0, blocking collectives: 96.3 us -> none  [the longest x4 82 us: grouped(): lax.all_to_all(value, 'atoms', split_axis=0, concat_axis=0, tiled=True, a...]
    all_to_all x2 -> x0, starting transfers between devices: 7.14 us -> none  [exchange(): lax.all_to_all(value, 'atoms', split_axis=0, concat_axis=0, tiled=True)]
  transfers between devices with their start and end apart: 2 -> 0, of which waited for: 2 -> 0; matrix products, arithmetic and copies ran while one was open for 1% -> 0% of each run, Pallas kernels for 1% -> 0%
where the time goes in v1:
time: 150 us
  Pallas kernels  140 us (93%)
  local copies, waits for them, and re-layouts  7.95 us (5%)
    pallas_call x1, Pallas kernels, local(): pl.pallas_call(body, out_shape=[jax.ShapeDtypeStruct((coefs, atoms, chann...  136 us
    pallas_call x1, Pallas kernels, local(): pl.pallas_call(spread_kernel, out_shape=[jax.ShapeDtypeStruct(w.shape, F3...  3.71 us

profile of v1, /device:TPU:0, one launch (start us, length us, event | category | flops | bytes accessed | tf_op | source)
XLA Modules:
  0.0 149.8 jit_solution(10612161905870729437)
XLA Ops:
  0.7 0.8 add_add_fusion
  1.4 0.8 copy.54
  2.2 0.1 reshape.520
  2.3 0.2 convert_reduce_fusion
  2.5 0.1 iota_compare_fusion
  2.6 0.1 add.348
  2.8 0.1 add.353
  2.9 0.8 copy.55
  3.7 0.1 copy.56
  3.8 0.1 select_reduce_fusion
  3.9 0.1 add.350
  4.1 0.1 copy.57
  4.2 0.1 convert_element_type.14
  4.3 0.1 fusion.10
  4.4 0.1 concatenate.4
  4.5 0.6 pad.4
  5.1 0.8 copy.60.refs_5_
  5.9 1.0 reshape.522
  6.9 0.8 copy.58
  7.7 0.8 copy.59
  8.5 136.0 %edges.1 = (bf16[9,128,128]{2,1,0:T(8,128)(2,1)}, f32[9,128,128]{2,1,0:T(8,128)}, bf16[512,16,128]{2,1,0:T(8,128)(2,1)}) custom-call(f32[32,1,128]{2,1,0:T(1,128)} %bitcast.21, bf16[9,128,128]{2,1,0:T(8,128)(2,1)} %bitcast.18, bf16[9,128,128]{2,1,0:T(8,128)(2,1)} %bitcast.19, f32[384,81]{1,0:T(8,128)} %bitcast.16, s32[384,2]{1,0:T(8,128)} %bitcast.15, ...), custom_call_target="tpu_custom_call" | custom-call | tf_op jit(solution)/shard_map/edges/pallas_call | solution.py:607
  144.5 3.7 %spread.1 = (f32[768,512]{1,0:T(8,128)}, f32[2,512,256]{2,1,0:T(8,128)}, f32[2,256,128]{2,1,0:T(8,128)}, f32[384,384]{1,0:T(8,128)}, f32[2,256,256]{2,1,0:T(8,128)}, /*index=5*/f32[2,128,128]{2,1,0:T(8,128)}) custom-call(bf16[8192,128]{1,0:T(8,128)(2,1)} %bitcast.14), custom_call_target="tpu_custom_call" | custom-call | tf_op jit(solution)/shard_map/spread/pallas_call | solution.py:622
  148.3 0.7 copy.63
  149.0 0.8 copy.64
  (16 shorter events, 0.3 us)
Async XLA Ops:
  144.5 3.7 %copy-start.1 = (bf16[9,128,128]{2,1,0:T(8,128)(2,1)S(1)}, bf16[9,128,128]{2,1,0:T(8,128)(2,1)}, u32[]{:S(2)}) copy-start(bf16[9,128,128]{2,1,0:T(8,128)(2,1)} %get-tuple-element.17) | copy-start | bytes 884740
  144.5 4.4 %copy-start = (f32[9,128,128]{2,1,0:T(8,128)S(1)}, f32[9,128,128]{2,1,0:T(8,128)}, u32[]{:S(2)}) copy-start(f32[9,128,128]{2,1,0:T(8,128)} %get-tuple-element.18) | copy-start | bytes 1769476

commit v2 on v1

--- a/solution.py
+++ b/solution.py
@@ -9,8 +9,15 @@
 DEGREES = ((0, 1), (1, 4), (4, 9))
 LANES = 128
 TILE = 16
-STREAMS = 4
-AT_ONCE = 31
+STREAMS = 8
+SKEW = 0
+PER_PIECE = 8
+AT_ONCE = 1
+PER_SEND = 1
+PER_EVENT = 0
+GROUPS = 2
+M_FIRST = 31
+M_PART = 4
 VMEM_BYTES = 66_000_000
 MESH = pl.DeviceIdType.MESH
 F32, BF16 = jnp.float32, jnp.bfloat16
@@ -65,34 +72,63 @@
     ref[rows:, cols:] = pair_ref[0]
 
 
-def spread_kernel(packed_ref, *out_refs):
+def final_kernel(weight_count, packed_ref, messages_ref, grads_ref, *refs):
+    messages_out, grads_out = refs[:2]
+    outs = refs[2 : 2 + weight_count]
+    staged = refs[2 + weight_count : 2 + 2 * weight_count]
+    sems = refs[-1]
+    pending = [
+        pltpu.make_async_copy(messages_ref, messages_out, sems.at[0]),
+        pltpu.make_async_copy(grads_ref, grads_out, sems.at[1]),
+    ]
+    for copy in pending:
+        copy.start()
     at = 0
-    for ref in out_refs:
+    for index, (ref, out) in enumerate(zip(staged, outs)):
         views = [ref] if len(ref.shape) == 2 else [ref.at[0], ref.at[1]]
         for view in views:
             height, width = view.shape
             for col in range(0, width, LANES):
-                view[:, col : col + LANES] = packed_ref[at : at + height, :].astype(F32)
+                rows = packed_ref[at // TILE : (at + height) // TILE]
+                view[:, col : col + LANES] = rows.reshape(height, LANES).astype(F32)
                 at += height
-
-
-def main_kernel(width, pair_chunk, per_pair, grad_scale, peers, *refs):
+        copy = pltpu.make_async_copy(ref, out, sems.at[2 + index])
+        copy.start()
+        pending.append(copy)
+    for copy in pending:
+        copy.wait()
+
+
+def main_kernel(width, pair_chunk, per_pair, grad_scale, peers, streams, *refs):
     (
-        req_ref, feat_ref, cot_ref, wig_ref, pos_ref, own_ref, fa0, fa1, fa2, sb0, sb1, sb2,
+        feat_in, cot_in, wig_in, *weights_in,
+        blocks_ref, pair_rows_ref, ends_ref,
         msg_ref, grad_ref, fin,
+        feat_ref, cot_ref, wig_raw, fa0, fa1, fa2, sb0, sb1, sb2,
         wa1, wa2, wb1, wb2,
-        asked, hots, mine, send_f, send_c, recv_f, recv_c, back_m, back_g,
+        req_ref, asked, hots, mine, wig_ref, pos_ref, send_f, send_c, recv_f, recv_c, back_m, back_g,
         pf, pc, am, ag,
         z, hid, gate_ref, act, dmix, dout, work, contrib,
         acc, snd, rcv,
-        req_s, req_r, f_s, f_r, c_s, c_r, m_s, m_r, g_s, g_r, w_s, w_r,
+        in_s, req_s, req_r, f_s, f_r, c_s, c_r, m_s, m_r, g_s, g_r, w_s, w_r,
     ) = refs
     shared = send_c is None
     send_c = send_f if shared else send_c
+    loads = [
+        pltpu.make_async_copy(source, target, in_s.at[i])
+        for i, (source, target) in enumerate(
+            zip(
+                (feat_in, cot_in, wig_in, *weights_in),
+                (feat_ref, cot_ref, wig_raw, fa0, fa1, fa2, sb0, sb1, sb2),
+            )
+        )
+    ]
+    for load in loads:
+        load.start()
     C = LANES
     coefs, atoms, _ = feat_ref.shape
     half = coefs * C
-    edges = wig_ref.shape[0]
+    edges = wig_raw.shape[2]
     pair_rows = pf.shape[0]
     parts = tile_parts(coefs, width)
     starts = unique(p[2] for p in parts)
@@ -108,6 +144,39 @@
         return carry
 
     lax.fori_loop(1, peers, greet, 0)
+
+    pairs = blocks_ref.shape[1]
+    row_width = pair_rows_ref.shape[0]
+    ranks = width // row_width
+    owners = blocks_ref[...].astype(F32)
+    earlier = lax.broadcasted_iota(jnp.int32, (pairs, pairs), 0) < lax.broadcasted_iota(
+        jnp.int32, (pairs, pairs), 1
+    )
+    peer_ids = lax.broadcasted_iota(jnp.int32, (peers, pairs), 0).astype(F32)
+    owned = [(peer_ids == owners[side : side + 1]).astype(F32) for side in (0, 1)]
+    count = dot_nn((owned[0] + owned[1]).astype(BF16), as_hot(earlier))
+    lane = lax.broadcasted_iota(jnp.int32, (row_width, C), 1)
+    member = lax.broadcasted_iota(jnp.int32, (row_width, C), 0)
+
+    def wanted_row(lanes):
+        flat = lanes % TILE
+        for s, start in enumerate(starts):
+            flat = jnp.where(lanes // TILE == s, flat + start, flat)
+        later = flat >= width
+        return jnp.where(later, flat - width, flat), later
+
+    row_at, _ = wanted_row(lane)
+    lanes_all = lax.broadcasted_iota(jnp.int32, (peers, C), 1)
+    _, second = wanted_row(lanes_all)
+    request = jnp.where(second, float(atoms), 0.0)
+    for k in range(ranks):
+        choose = as_hot((row_at == member + k * row_width) & (lane < TILE * len(starts)))
+        for side in (0, 1):
+            rows = dot_tn(pair_rows_ref[:, side, :].astype(F32).astype(BF16), choose)
+            holder = jnp.where(count == float(k), owned[side], 0.0)
+            request = request + dot_nn(holder.astype(BF16), rows.astype(BF16))
+    req_ref[...] = request.reshape(peers, 1, C)
+
     pl.semaphore_wait(barrier, peers - 1)
 
     def copies(source, target, send_sem, recv_sem):
@@ -141,26 +210,16 @@
     start_req, wait_req = copies(req_ref, asked, req_s, req_r)
     start_req()
     asked[me] = req_ref[me]
-    widen_into(wa1, fa1)
-    widen_into(wa2, fa2)
-    widen_into(wb1, sb1)
-    widen_into(wb2, sb2)
-    base = 0
-    for m, off in enumerate(kinds):
-        span = slots * (1 + (off + width - 1) // TILE)
-        ids = lax.broadcasted_iota(jnp.int32, (pair_rows, span), 1)
-        mine[:, base : base + span] = as_hot(own_ref[:, m : m + 1] == ids)
-        base += span
     wait_req()
 
     rows_of = lax.broadcasted_iota(jnp.int32, (slots, peers), 0) // TILE
     chooser = as_hot(rows_of == lax.broadcasted_iota(jnp.int32, (slots, peers), 1))
     wanted = dot_nn(chooser, asked[...].reshape(peers, C).astype(BF16))
-    lane = lax.broadcasted_iota(jnp.int32, (slots, C), 1)
+    slot_lane = lax.broadcasted_iota(jnp.int32, (slots, C), 1)
     inner = lax.broadcasted_iota(jnp.int32, (slots, C), 0) % TILE
     atom_ids = lax.broadcasted_iota(jnp.int32, (slots, 2 * atoms), 1).astype(F32)
     for s in range(len(starts)):
-        column = jnp.sum(jnp.where(lane == inner + s * TILE, wanted, 0.0), axis=1, keepdims=True)
+        column = jnp.sum(jnp.where(slot_lane == inner + s * TILE, wanted, 0.0), axis=1, keepdims=True)
         hots[s] = as_hot(column == atom_ids)
 
     def pick(block_ref, out_ref):
@@ -173,14 +232,76 @@
 
     start_f, wait_f = copies(send_f, recv_f, f_s, f_r)
     start_c, wait_c = copies(send_c, recv_c, c_s, c_r)
+    loads[0].wait()
     pick(feat_ref, send_f)
     start_f()
     recv_f[me] = send_f[me]
     if shared:
         wait_f()
+    loads[1].wait()
     pick(cot_ref, send_c)
     start_c()
     recv_c[me] = send_c[me]
+
+    own = None
+    end_row = lax.broadcasted_iota(jnp.int32, (pair_rows, pairs), 0)
+    first_row = lax.broadcasted_iota(jnp.int32, (pair_rows, pairs), 1) * (2 * row_width)
+    row_ids = lax.broadcasted_iota(jnp.int32, (8, pairs), 0)
+    for side in (0, 1):
+        low = first_row + side * row_width
+        inside = (end_row >= low) & (end_row < low + row_width)
+        shift = jnp.where(inside, end_row - low, 0)
+        held = jnp.sum(owned[side] * count, axis=0, keepdims=True)
+        known = jnp.where(row_ids == 0, owners[side : side + 1], jnp.where(row_ids == 1, held, 0.0))
+        known = jnp.where(row_ids == 2, 1.0, known)
+        term = lax.dot_general(
+            as_hot(inside), known.astype(BF16), (((1,), (1,)), ((), ())), preferred_element_type=F32
+        )
+        term = jnp.concatenate(
+            [term[:, :2], jnp.sum(shift.astype(F32), axis=1, keepdims=True)], axis=1
+        )
+        own = term if own is None else own + term
+    in_slot = own[:, 1:2] * float(row_width) + own[:, 2:3]
+    base = 0
+    for off in kinds:
+        tiles = 1 + (off + width - 1) // TILE
+        place = in_slot + float(off)
+        place = jnp.where(place >= float(TILE), place + float(slots - TILE), place)
+        place = place + own[:, 0:1] * float(TILE)
+        ids = lax.broadcasted_iota(jnp.int32, (pair_rows, tiles * slots), 1).astype(F32)
+        mine[:, base : base + tiles * slots] = as_hot(place == ids)
+        base += tiles * slots
+
+    for load in loads[2:]:
+        load.wait()
+    diagonal = lax.broadcasted_iota(jnp.int32, (edges, edges), 0) == lax.broadcasted_iota(
+        jnp.int32, (edges, edges), 1
+    )
+    unit = diagonal.astype(F32)
+    for i in range(coefs):
+        turned = lax.dot_general(
+            unit, wig_raw[i], (((1,), (1,)), ((), ())),
+            precision=lax.Precision.HIGHEST, preferred_element_type=F32,
+        )
+        wig_ref[:, i * coefs : (i + 1) * coefs] = turned
+    ends = lax.dot_general(
+        as_hot(diagonal), ends_ref[...].astype(F32).astype(BF16), (((1,), (1,)), ((), ())),
+        preferred_element_type=F32,
+    )
+    pair_base = None
+    edge_ids = lax.broadcasted_iota(jnp.int32, (edges, 1), 0)
+    for p in range(edges // per_pair):
+        step = jnp.where(edge_ids >= p * per_pair, float(2 * row_width), 0.0)
+        if p and p % pair_chunk == 0:
+            step = jnp.where(edge_ids >= p * per_pair, float(2 * row_width * (1 - pair_chunk)), 0.0)
+        pair_base = jnp.zeros_like(step) if pair_base is None else pair_base + step
+    pos_ref[...] = ends + pair_base + jnp.where(
+        lax.broadcasted_iota(jnp.int32, (edges, 2), 1) == 1, float(row_width), 0.0
+    )
+    widen_into(wa1, fa1)
+    widen_into(wa2, fa2)
+    widen_into(wb1, sb1)
+    widen_into(wb2, sb2)
 
     def own_hot(j):
         m = kinds.index(offsets[j])
@@ -218,7 +339,7 @@
 
     def hot_of(index):
         span = pl.ds(pl.multiple_of(index * chunk, chunk), chunk)
-        ids = lax.broadcasted_iota(jnp.int32, (chunk, locals_), 1)
+        ids = lax.broadcasted_iota(jnp.int32, (chunk, locals_), 1).astype(F32)
         return jnp.concatenate(
             [as_hot(pos_ref[span, side : side + 1] == ids) for side in (0, 1)], axis=0
         )
@@ -305,15 +426,19 @@
         unrotate(index, hot, take, am)
         return carry
 
-    def backward(index, carry):
+    def backward_first(index, carry):
         hot = hot_of(index)
-        hc, gc, dc, oc = (r.at[all_rows(index)] for r in (hid, gate_ref, dmix, dout))
+        dc = dmix.at[all_rows(index)]
 
         def put(i, ct, cs):
             dc[T, i * C : (i + 1) * C] = ct
             dc[S, i * C : (i + 1) * C] = cs
 
         rotate(index, hot, pc, put)
+        return carry
+
+    def backward(index, carry):
+        hc, gc, dc, oc = (r.at[all_rows(index)] for r in (hid, gate_ref, dmix, dout))
         dact = work
         dact[:, : 3 * C] = dot_nt(dc[:, : 3 * C], sb0[...])
         dact[:, 3 * C : 7 * C] = dot_nt(dc[:, 3 * C : 7 * C], wb1[...])
@@ -338,6 +463,7 @@
         work[:, : 6 * C] = dot_nt(oc[:, : 4 * C], fa0[...])
         work[:, 6 * C : 14 * C] = dot_nt(oc[:, 4 * C : 8 * C], wa1[...])
         work[:, 14 * C :] = dot_nt(oc[:, 8 * C :], wa2[...])
+        advance(PER_PIECE)
 
         def take(i):
             left = slice(2 * i * C, (2 * i + 1) * C)
@@ -356,55 +482,48 @@
     start_m, wait_m = copies(ret_m, back_m, m_s, m_r)
     start_g, wait_g = copies(ret_g, back_g, g_s, g_r)
     scatter(am, ret_m)
-    start_m()
     back_m[me] = ret_m[me]
+    returns = [(start, k) for start in (start_m, start_g) for k in range(1, peers)]
+    grads_ready = [False]
+    portion = max(1, (peers - 1) // 31)
+
+    def give(number):
+        number *= portion
+        while number > 0 and returns:
+            start, first = returns[0]
+            if start is start_g and not grads_ready[0]:
+                return
+            last = first
+            while returns and returns[0][0] is start and last - first < number:
+                last = returns.pop(0)[1] + 1
+            start(first, last)
+            number -= last - first
+
+    give(M_FIRST)
 
     wait_c()
+    give(M_PART)
     gather(recv_c, pc)
-    lax.fori_loop(0, chunks, backward, 0)
-
-    at = 0
-
-    def put(value):
-        nonlocal at
-        height = value.shape[0]
-        for col in range(0, value.shape[1], C):
-            acc[at // TILE : (at + height) // TILE] = value[:, col : col + C].reshape(height // TILE, TILE, C)
-            at += height
-
-    def weight_pair(left, right):
-        rows, cols = left.shape[1] // 2, right.shape[1] // 2
-        upper = dot_tn(left[:, :rows], right)
-        lower = dot_tn(left[:, rows:], right)
-        put(upper[:, :cols] + lower[:, cols:])
-        put(upper[:, cols:] - lower[:, :cols])
-
-    put(dot_tn(z[:, : 6 * C], dout[:, : 4 * C]))
-    weight_pair(z[:, 6 * C : 14 * C], dout[:, 4 * C : 8 * C])
-    weight_pair(z[:, 14 * C :], dout[:, 8 * C :])
-    put(dot_tn(act[:, : 3 * C], dmix[:, : 3 * C]))
-    weight_pair(act[:, 3 * C : 7 * C], dmix[:, 3 * C : 7 * C])
-    weight_pair(act[:, 7 * C :], dmix[:, 7 * C :])
+    lax.fori_loop(0, chunks, backward_first, 0)
+    give(M_PART)
+
     blocks = acc.shape[0]
-    if at < blocks * TILE:
-        acc[at // TILE :] = jnp.zeros((blocks - at // TILE, TILE, C), F32)
-
     bits = peers.bit_length() - 1
-    stream = blocks // STREAMS
+    stream = blocks // streams
     core = lax.rem(me, 2)
     strides = [2**b for b in range(bits)]
     if bits >= 3:
         strides[1] = 2 + 2 * core
         strides[2] = 4 - 2 * core
-    low = [q * stream for q in range(STREAMS)]
+    low = [q * stream for q in range(streams)]
 
     def w_copy(source, target, q, stage, stride):
         bit = lax.rem(me // stride, 2)
         return pltpu.make_async_remote_copy(
             src_ref=source,
             dst_ref=target,
-            send_sem=w_s.at[stage * STREAMS + q],
-            recv_sem=w_r.at[stage * STREAMS + q],
+            send_sem=w_s.at[stage * streams + q],
+            recv_sem=w_r.at[stage * streams + q],
             device_id=(me + stride * (1 - 2 * bit),),
             device_id_type=MESH,
         )
@@ -443,42 +562,77 @@
         bit = lax.rem(me // strides[stage], 2)
         low[q] = low[q] - bit * size
 
-    states = [halve_start(q, 0) for q in range(STREAMS)]
-
-    def half_step(stage):
-        for q in range(STREAMS):
-            halve_end(q, stage, states[q])
-            if stage + 1 < bits:
-                states[q] = halve_start(q, stage + 1)
-            else:
-                states[q] = double_start(q, stage)
-            send_some()
-
-    def whole_step(stage):
-        for q in range(STREAMS):
+    states = [None] * streams
+    events = sorted(
+        ((q * GROUPS // streams * SKEW + s, q, s) for q in range(streams) for s in range(2 * bits)), reverse=True
+    )
+
+    def step(q, s):
+        if s < bits:
+            halve_end(q, s, states[q])
+            states[q] = halve_start(q, s + 1) if s + 1 < bits else double_start(q, s)
+        else:
+            stage = 2 * bits - 1 - s
             double_end(q, stage, states[q])
             if stage:
                 states[q] = double_start(q, stage - 1)
-            send_some()
-
-    sent = [0]
-
-    def send_some():
-        if sent[0]:
-            last = min(peers, sent[0] + AT_ONCE * (peers - 1) // 31)
-            start_g(sent[0], last)
-            sent[0] = last
+
+    started = [0]
+
+    def advance(number):
+        for _ in range(number):
+            if events and events[-1][1] < started[0]:
+                _, q, s = events.pop()
+                step(q, s)
+                give(PER_EVENT)
+
+    at = 0
+
+    def put(value):
+        nonlocal at
+        height = value.shape[0]
+        for col in range(0, value.shape[1], C):
+            acc[at // TILE : (at + height) // TILE] = value[:, col : col + C].reshape(height // TILE, TILE, C)
+            at += height
+        begin()
+
+    def begin():
+        while started[0] < streams and (started[0] + 1) * stream * TILE <= at:
+            states[started[0]] = halve_start(started[0], 0)
+            started[0] += 1
+
+    def weight_pair(left, right):
+        rows, cols = left.shape[1] // 2, right.shape[1] // 2
+        upper = dot_tn(left[:, :rows], right)
+        lower = dot_tn(left[:, rows:], right)
+        put(upper[:, :cols] + lower[:, cols:])
+        put(upper[:, cols:] - lower[:, :cols])
+
+    put(dot_tn(act[:, : 3 * C], dmix[:, : 3 * C]))
+    weight_pair(act[:, 3 * C : 7 * C], dmix[:, 3 * C : 7 * C])
+    weight_pair(act[:, 7 * C :], dmix[:, 7 * C :])
+    give(M_PART)
+    lax.fori_loop(0, chunks, backward, 0)
+    give(M_PART)
+    put(dot_tn(z[:, : 6 * C], dout[:, : 4 * C]))
+    advance(PER_PIECE)
+    weight_pair(z[:, 6 * C : 14 * C], dout[:, 4 * C : 8 * C])
+    advance(PER_PIECE)
+    weight_pair(z[:, 14 * C :], dout[:, 8 * C :])
+    if at < blocks * TILE:
+        acc[at // TILE :] = jnp.zeros((blocks - at // TILE, TILE, C), F32)
+        at = blocks * TILE
+        begin()
 
     for index in range(chunks):
         inputs_grad(index, 0)
-        if index < bits - 1:
-            half_step(index)
+        advance(PER_PIECE)
     scatter(ag, ret_g)
     back_g[me] = ret_g[me]
-    sent[0] = 1
-    send_some()
-    for stage in range(min(chunks, bits - 1), bits):
-        half_step(stage)
+    grads_ready[0] = True
+    while returns:
+        give(AT_ONCE)
+        advance(PER_SEND)
 
     def collect(back, out, dtype):
         for j in range(coefs):
@@ -492,14 +646,9 @@
                 total = term if total is None else total + term
             out[j] = total.astype(dtype)
 
-    stages = list(reversed(range(bits)))
-    whole_step(stages[0])
-    while sent[0] < peers:
-        send_some()
     wait_m()
     collect(back_m, msg_ref, BF16)
-    for stage in stages[1:]:
-        whole_step(stage)
+    advance(len(events))
     wait_g()
     collect(back_g, grad_ref, F32)
 
@@ -516,47 +665,14 @@
     half = coefs * channels
     bits = peers.bit_length() - 1
 
-    owners = pair_blocks.reshape(2 * pair_count)
-    spots = jnp.arange(2 * pair_count, dtype=jnp.int32)
-    rank = jnp.sum(
-        (owners[:, None] == owners[None, :]) & (spots[:, None] > spots[None, :]), axis=1
-    ).astype(jnp.int32)
-    end_rows = jnp.transpose(pair_rows, (2, 0, 1)).reshape(2 * pair_count, row_width)
-    place = owners * slot_count + rank
-    names = jnp.arange(peers * slot_count, dtype=jnp.int32)
-    request = jnp.sum(
-        jnp.where((place[None, :] == names[:, None])[:, :, None], end_rows[None], 0), axis=1
-    ).astype(F32)
-    request = request.reshape(peers, width)
-
     parts = tile_parts(coefs, width)
     starts = unique(p[2] for p in parts)
-    pieces = []
-    for start in starts:
-        pieces.append(request[:, start:][:, :TILE])
-        left = TILE - (width - start)
-        if left > 0:
-            pieces.append(request[:, :left] + float(atoms))
-    asked = jnp.concatenate(pieces, axis=1)
-    asked = jnp.pad(asked, ((0, 0), (0, LANES - asked.shape[1]))).reshape(peers, 1, LANES)
-
     kinds = unique(own_offsets(coefs, width))
-    row_in_slot = rank[:, None] * row_width + jnp.arange(row_width, dtype=jnp.int32)[None, :]
-    owned = []
-    for off in kinds:
-        at = row_in_slot + off
-        owned.append((at // TILE) * (peers * TILE) + owners[:, None] * TILE + at % TILE)
-    own = jnp.stack(owned, axis=-1).reshape(2 * pair_count * row_width, len(kinds))
-
     crowded = peers > 64
     pair_chunk = pair_count // (4 if crowded else 2)
-    in_chunk = jnp.arange(edges, dtype=jnp.int32) // per_pair % pair_chunk * (2 * row_width)
-    positions = jnp.transpose(edge_ends) + in_chunk[:, None]
-    positions = positions + jnp.array([[0, row_width]], dtype=jnp.int32)
-    wig = jnp.transpose(wigner.reshape(coefs * coefs, edges))
-
     total_rows = sum(w.size for w in weights) // LANES
-    unit = TILE * peers * STREAMS
+    streams = 4 if crowded else STREAMS
+    unit = TILE * peers * streams
     packed_rows = -(-total_rows // unit) * unit
     rows = 2 * edges
     chunk_rows = 2 * pair_chunk * per_pair
@@ -569,10 +685,17 @@
     end_count = 2 * pair_count * row_width
     packed_blocks = (packed_rows // TILE, TILE, LANES)
     scratch = [
+        V((coefs, atoms, channels), BF16),
+        V((coefs, atoms, channels), BF16),
+        V((coefs, coefs, edges), F32),
+        *[V(w.shape, BF16) for w in weights],
         *[V(shape, BF16) for shape in wide],
+        V((peers, 1, LANES), F32),
         V((peers, 1, LANES), F32),
         V((len(starts), slots, 2 * atoms), BF16),
         V((end_count, mine_width), BF16),
+        V((edges, coefs * coefs), F32),
+        V((edges, 2), F32),
         *[V(block, BF16) for _ in range(5 if crowded else 6)],
         *[V((end_count, half), BF16) for _ in range(4)],
         V((rows, 2 * half), BF16),
@@ -586,24 +709,22 @@
         V(packed_blocks, F32),
         V(packed_blocks, BF16),
         V(packed_blocks, BF16),
+        DMA((3 + len(weights),)),
         *[DMA((peers,)) for _ in range(10)],
-        DMA((2 * bits * STREAMS,)),
-        DMA((2 * bits * STREAMS,)),
+        DMA((2 * bits * streams,)),
+        DMA((2 * bits * streams,)),
     ]
     whole = pl.BlockSpec(memory_space=pltpu.VMEM)
-    first_block = 15 + 4 + 3
+    first_block = 15 + 9 + 4 + 6
     grad_scale = (2.0 * edges * peers) ** (-0.5)
 
     def body(*refs):
         refs = list(refs)
         if crowded:
             refs.insert(first_block + 1, None)
-        main_kernel(width, pair_chunk, per_pair, grad_scale, peers, *refs)
-
-    operands = (
-        asked, jnp.transpose(features, (1, 0, 2)), jnp.transpose(cotangent, (1, 0, 2)),
-        wig, positions, own, *weights,
-    )
+        main_kernel(width, pair_chunk, per_pair, grad_scale, peers, streams, *refs)
+
+    anywhere = pl.BlockSpec(memory_space=pl.ANY)
     messages, grads, packed = pl.pallas_call(
         body,
         out_shape=[
@@ -611,22 +732,35 @@
             jax.ShapeDtypeStruct((coefs, atoms, channels), F32),
             jax.ShapeDtypeStruct(packed_blocks, BF16),
         ],
-        in_specs=[whole] * len(operands),
+        in_specs=[anywhere] * (3 + len(weights)) + [whole] * 3,
         out_specs=[whole] * 3,
         scratch_shapes=scratch,
         compiler_params=pltpu.CompilerParams(
             collective_id=0, has_side_effects=True, vmem_limit_bytes=VMEM_BYTES
         ),
         name="edges",
-    )(*operands)
-    outs = pl.pallas_call(
-        spread_kernel,
-        out_shape=[jax.ShapeDtypeStruct(w.shape, F32) for w in weights],
-        in_specs=[whole],
-        out_specs=[whole] * len(weights),
+    )(
+        jnp.transpose(features, (1, 0, 2)), jnp.transpose(cotangent, (1, 0, 2)), wigner, *weights,
+        jnp.transpose(pair_blocks), jnp.transpose(pair_rows, (1, 0, 2)), edge_ends,
+    )
+    ordered = (second_m0, second_m1, second_m2, first_m0, first_m1, first_m2)
+
+    def final(*refs):
+        final_kernel(len(ordered), *refs)
+
+    shapes = [jax.ShapeDtypeStruct(w.shape, F32) for w in ordered]
+    messages, grads, *outs = pl.pallas_call(
+        final,
+        out_shape=[
+            jax.ShapeDtypeStruct(messages.shape, BF16), jax.ShapeDtypeStruct(grads.shape, F32), *shapes
+        ],
+        in_specs=[whole] * 3,
+        out_specs=[anywhere] * (2 + len(ordered)),
+        scratch_shapes=[*[V(w.shape, F32) for w in ordered], DMA((2 + len(ordered),))],
         compiler_params=pltpu.CompilerParams(vmem_limit_bytes=VMEM_BYTES),
-        name="spread",
-    )(packed.reshape(packed_rows, LANES))
+        name="finish",
+    )(packed, messages, grads)
+    outs = (*outs[3:], *outs[:3])
     return (jnp.transpose(messages, (1, 0, 2)), jnp.transpose(grads, (1, 0, 2)), *outs)
 
 

time: 150 us -> 127 us (0.85)
  Pallas kernels: 140 us -> 126 us
  local copies, waits for them, and re-layouts: 7.95 us -> 0 us
    pallas_call x1, Pallas kernels: 136 us -> 122 us  [local(): pl.pallas_call(body, out_shape=[jax.ShapeDtypeStruct((coefs, atoms, chann...]
    unnamed x7 -> x0, local copies, waits for them, and re-layouts: 2.29 us -> none
    reshape x3 -> x0, local copies, waits for them, and re-layouts: 1.86 us -> none  [the longest x2 1.78 us: local(): wig = jnp.transpose(wigner.reshape(coefs * coefs, edges))]
where the time goes in v2:
time: 127 us
  Pallas kernels  126 us (99%)
    pallas_call x1, Pallas kernels, local(): pl.pallas_call(body, out_shape=[jax.ShapeDtypeStruct((coefs, atoms, chann...  122 us
    pallas_call x1, Pallas kernels, local(): pl.pallas_call(final, out_shape=[jax.ShapeDtypeStruct(messages.shape, BF1...  4.12 us

profile of v2, /device:TPU:0, one launch (start us, length us, event | category | flops | bytes accessed | tf_op | source)
XLA Modules:
  0.0 126.8 jit_solution(16535989225099642256)
XLA Ops:
  0.6 121.9 %edges.1 = (bf16[9,128,128]{2,1,0:T(8,128)(2,1)}, f32[9,128,128]{2,1,0:T(8,128)}, bf16[512,16,128]{2,1,0:T(8,128)(2,1)}) custom-call(bf16[9,128,128]{2,1,0:T(8,128)(2,1)} %bitcast.6, bf16[9,128,128]{2,1,0:T(8,128)(2,1)} %bitcast.7, f32[9,9,384]{2,1,0:T(8,128)} %refs_2_.1, bf16[768,512]{1,0:T(8,128)(2,1)} %refs_3_.1, bf16[2,512,256]{2,1,0:T(8,128)(2,1)} %refs_4_.1, ...), custom_call_target="tpu_custom_call" | custom-call | tf_op jit(solution)/shard_map/edges/pallas_call | solution.py:728
  122.5 4.1 %finish.1 = (bf16[9,128,128]{2,1,0:T(8,128)(2,1)}, f32[9,128,128]{2,1,0:T(8,128)}, f32[384,384]{1,0:T(8,128)}, f32[2,256,256]{2,1,0:T(8,128)}, f32[2,128,128]{2,...) custom-call(bf16[512,16,128]{2,1,0:T(8,128)(2,1)} %get-tuple-element.19.refs_0_, ...), custom_call_target="tpu_custom_call" | custom-call | tf_op jit(solution)/shard_map/finish/pallas_call | solution.py:752

commit v3 on v2

--- a/solution.py
+++ b/solution.py
@@ -10,6 +10,8 @@
 LANES = 128
 TILE = 16
 STREAMS = 8
+STRIDE = 11
+BEFORE = 0
 SKEW = 0
 PER_PIECE = 8
 AT_ONCE = 1
@@ -72,11 +74,21 @@
     ref[rows:, cols:] = pair_ref[0]
 
 
-def final_kernel(weight_count, packed_ref, messages_ref, grads_ref, *refs):
+def final_kernel(weight_count, packed_in, messages_ref, grads_ref, *refs):
     messages_out, grads_out = refs[:2]
     outs = refs[2 : 2 + weight_count]
     staged = refs[2 + weight_count : 2 + 2 * weight_count]
-    sems = refs[-1]
+    packed_ref, sems = refs[-2:]
+    loads = []
+    at = 0
+    for index, ref in enumerate(staged):
+        blocks = ref.size // (TILE * LANES)
+        span = pl.ds(at, blocks)
+        loads.append(
+            pltpu.make_async_copy(packed_in.at[span], packed_ref.at[span], sems.at[2 + weight_count + index])
+        )
+        loads[-1].start()
+        at += blocks
     pending = [
         pltpu.make_async_copy(messages_ref, messages_out, sems.at[0]),
         pltpu.make_async_copy(grads_ref, grads_out, sems.at[1]),
@@ -85,6 +97,7 @@
         copy.start()
     at = 0
     for index, (ref, out) in enumerate(zip(staged, outs)):
+        loads[index].wait()
         views = [ref] if len(ref.shape) == 2 else [ref.at[0], ref.at[1]]
         for view in views:
             height, width = view.shape
@@ -103,6 +116,7 @@
     (
         feat_in, cot_in, wig_in, *weights_in,
         blocks_ref, pair_rows_ref, ends_ref,
+        msg_out, grad_out, fin_out,
         msg_ref, grad_ref, fin,
         feat_ref, cot_ref, wig_raw, fa0, fa1, fa2, sb0, sb1, sb2,
         wa1, wa2, wb1, wb2,
@@ -110,7 +124,7 @@
         pf, pc, am, ag,
         z, hid, gate_ref, act, dmix, dout, work, contrib,
         acc, snd, rcv,
-        in_s, req_s, req_r, f_s, f_r, c_s, c_r, m_s, m_r, g_s, g_r, w_s, w_r,
+        in_s, out_s, req_s, req_r, f_s, f_r, c_s, c_r, m_s, m_r, g_s, g_r, w_s, w_r,
     ) = refs
     shared = send_c is None
     send_c = send_f if shared else send_c
@@ -181,7 +195,7 @@
 
     def copies(source, target, send_sem, recv_sem):
         def at(k):
-            to = lax.rem(me + k, peers)
+            to = lax.rem(me + k * STRIDE, peers)
             return pltpu.make_async_remote_copy(
                 src_ref=source.at[to],
                 dst_ref=target.at[me],
@@ -563,6 +577,7 @@
         low[q] = low[q] - bit * size
 
     states = [None] * streams
+    pending = []
     events = sorted(
         ((q * GROUPS // streams * SKEW + s, q, s) for q in range(streams) for s in range(2 * bits)), reverse=True
     )
@@ -576,6 +591,10 @@
             double_end(q, stage, states[q])
             if stage:
                 states[q] = double_start(q, stage - 1)
+            else:
+                span = pl.ds(q * stream, stream)
+                pending.append(pltpu.make_async_copy(fin.at[span], fin_out.at[span], out_s.at[2 + q]))
+                pending[-1].start()
 
     started = [0]
 
@@ -630,6 +649,7 @@
     scatter(ag, ret_g)
     back_g[me] = ret_g[me]
     grads_ready[0] = True
+    advance(BEFORE)
     while returns:
         give(AT_ONCE)
         advance(PER_SEND)
@@ -648,9 +668,15 @@
 
     wait_m()
     collect(back_m, msg_ref, BF16)
+    pending.append(pltpu.make_async_copy(msg_ref, msg_out, out_s.at[0]))
+    pending[-1].start()
     advance(len(events))
     wait_g()
     collect(back_g, grad_ref, F32)
+    pending.append(pltpu.make_async_copy(grad_ref, grad_out, out_s.at[1]))
+    pending[-1].start()
+    for copy in pending:
+        copy.wait()
 
 
 def local(features, cotangent, wigner, pair_blocks, pair_rows, edge_ends, *weights):
@@ -685,6 +711,9 @@
     end_count = 2 * pair_count * row_width
     packed_blocks = (packed_rows // TILE, TILE, LANES)
     scratch = [
+        V((coefs, atoms, channels), BF16),
+        V((coefs, atoms, channels), F32),
+        V(packed_blocks, BF16),
         V((coefs, atoms, channels), BF16),
         V((coefs, atoms, channels), BF16),
         V((coefs, coefs, edges), F32),
@@ -710,12 +739,13 @@
         V(packed_blocks, BF16),
         V(packed_blocks, BF16),
         DMA((3 + len(weights),)),
+        DMA((2 + streams,)),
         *[DMA((peers,)) for _ in range(10)],
         DMA((2 * bits * streams,)),
         DMA((2 * bits * streams,)),
     ]
     whole = pl.BlockSpec(memory_space=pltpu.VMEM)
-    first_block = 15 + 9 + 4 + 6
+    first_block = 15 + 3 + 9 + 4 + 6
     grad_scale = (2.0 * edges * peers) ** (-0.5)
 
     def body(*refs):
@@ -733,7 +763,7 @@
             jax.ShapeDtypeStruct(packed_blocks, BF16),
         ],
         in_specs=[anywhere] * (3 + len(weights)) + [whole] * 3,
-        out_specs=[whole] * 3,
+        out_specs=[anywhere] * 3,
         scratch_shapes=scratch,
         compiler_params=pltpu.CompilerParams(
             collective_id=0, has_side_effects=True, vmem_limit_bytes=VMEM_BYTES
@@ -754,9 +784,11 @@
         out_shape=[
             jax.ShapeDtypeStruct(messages.shape, BF16), jax.ShapeDtypeStruct(grads.shape, F32), *shapes
         ],
-        in_specs=[whole] * 3,
+        in_specs=[anywhere, whole, whole],
         out_specs=[anywhere] * (2 + len(ordered)),
-        scratch_shapes=[*[V(w.shape, F32) for w in ordered], DMA((2 + len(ordered),))],
+        scratch_shapes=[
+            *[V(w.shape, F32) for w in ordered], V(packed.shape, BF16), DMA((2 + 2 * len(ordered),))
+        ],
         compiler_params=pltpu.CompilerParams(vmem_limit_bytes=VMEM_BYTES),
         name="finish",
     )(packed, messages, grads)

time: 127 us -> 126 us (level)
    pallas_call x1, Pallas kernels: 122 us -> 120 us  [local(): pl.pallas_call(body, out_shape=[jax.ShapeDtypeStruct((coefs, atoms, chann...]
where the time goes in v3:
time: 126 us
  Pallas kernels  125 us (99%)
    pallas_call x1, Pallas kernels, local(): pl.pallas_call(body, out_shape=[jax.ShapeDtypeStruct((coefs, atoms, chann...  120 us
    pallas_call x1, Pallas kernels, local(): pl.pallas_call(final, out_shape=[jax.ShapeDtypeStruct(messages.shape, BF1...  4.7 us

profile of v3, /device:TPU:0, one launch (start us, length us, event | category | flops | bytes accessed | tf_op | source)
XLA Modules:
  0.0 125.9 jit_solution(2258519800441121321)
XLA Ops:
  0.6 120.4 %edges.1 = (bf16[9,128,128]{2,1,0:T(8,128)(2,1)}, f32[9,128,128]{2,1,0:T(8,128)}, bf16[512,16,128]{2,1,0:T(8,128)(2,1)}) custom-call(bf16[9,128,128]{2,1,0:T(8,128)(2,1)} %bitcast.6, bf16[9,128,128]{2,1,0:T(8,128)(2,1)} %bitcast.7, f32[9,9,384]{2,1,0:T(8,128)} %refs_2_.1, bf16[768,512]{1,0:T(8,128)(2,1)} %refs_3_.1, bf16[2,512,256]{2,1,0:T(8,128)(2,1)} %refs_4_.1, ...), custom_call_target="tpu_custom_call" | custom-call | tf_op jit(solution)/shard_map/edges/pallas_call | solution.py:758
  121.1 4.7 %finish.1 = (bf16[9,128,128]{2,1,0:T(8,128)(2,1)}, f32[9,128,128]{2,1,0:T(8,128)}, f32[384,384]{1,0:T(8,128)}, f32[2,256,256]{2,1,0:T(8,128)}, f32[2,128,128]{2,...) custom-call(bf16[512,16,128]{2,1,0:T(8,128)(2,1)} %get-tuple-element.19.refs_0_, ...), custom_call_target="tpu_custom_call" | custom-call | tf_op jit(solution)/shard_map/finish/pallas_call | solution.py:782

commit v4 on v3

--- a/solution.py
+++ b/solution.py
@@ -648,12 +648,6 @@
         advance(PER_PIECE)
     scatter(ag, ret_g)
     back_g[me] = ret_g[me]
-    grads_ready[0] = True
-    advance(BEFORE)
-    while returns:
-        give(AT_ONCE)
-        advance(PER_SEND)
-
     def collect(back, out, dtype):
         for j in range(coefs):
             total = None
@@ -666,10 +660,18 @@
                 total = term if total is None else total + term
             out[j] = total.astype(dtype)
 
-    wait_m()
-    collect(back_m, msg_ref, BF16)
-    pending.append(pltpu.make_async_copy(msg_ref, msg_out, out_s.at[0]))
-    pending[-1].start()
+    grads_ready[0] = True
+    advance(BEFORE)
+    collected = False
+    while returns:
+        give(AT_ONCE)
+        advance(PER_SEND)
+        if not collected and len(returns) <= peers // 2:
+            collected = True
+            wait_m()
+            collect(back_m, msg_ref, BF16)
+            pending.append(pltpu.make_async_copy(msg_ref, msg_out, out_s.at[0]))
+            pending[-1].start()
     advance(len(events))
     wait_g()
     collect(back_g, grad_ref, F32)

time: 126 us -> 126 us (level)
  no operation moved by 1% of the time
where the time goes in v4:
time: 126 us
  Pallas kernels  125 us (99%)
    pallas_call x1, Pallas kernels, local(): pl.pallas_call(body, out_shape=[jax.ShapeDtypeStruct((coefs, atoms, chann...  120 us
    pallas_call x1, Pallas kernels, local(): pl.pallas_call(final, out_shape=[jax.ShapeDtypeStruct(messages.shape, BF1...  4.7 us

profile of v4, /device:TPU:0, one launch (start us, length us, event | category | flops | bytes accessed | tf_op | source)
XLA Modules:
  0.0 125.9 jit_solution(6890130506869222698)
XLA Ops:
  0.6 120.4 %edges.1 = (bf16[9,128,128]{2,1,0:T(8,128)(2,1)}, f32[9,128,128]{2,1,0:T(8,128)}, bf16[512,16,128]{2,1,0:T(8,128)(2,1)}) custom-call(bf16[9,128,128]{2,1,0:T(8,128)(2,1)} %bitcast.6, bf16[9,128,128]{2,1,0:T(8,128)(2,1)} %bitcast.7, f32[9,9,384]{2,1,0:T(8,128)} %refs_2_.1, bf16[768,512]{1,0:T(8,128)(2,1)} %refs_3_.1, bf16[2,512,256]{2,1,0:T(8,128)(2,1)} %refs_4_.1, ...), custom_call_target="tpu_custom_call" | custom-call | tf_op jit(solution)/shard_map/edges/pallas_call | solution.py:760
  121.1 4.7 %finish.1 = (bf16[9,128,128]{2,1,0:T(8,128)(2,1)}, f32[9,128,128]{2,1,0:T(8,128)}, f32[384,384]{1,0:T(8,128)}, f32[2,256,256]{2,1,0:T(8,128)}, f32[2,128,128]{2,...) custom-call(bf16[512,16,128]{2,1,0:T(8,128)(2,1)} %get-tuple-element.19.refs_0_, ...), custom_call_target="tpu_custom_call" | custom-call | tf_op jit(solution)/shard_map/finish/pallas_call | solution.py:784
